TPU v7x, 128 devices: a whole 4x4x4 slice. The times are simulated.
128 devices in a mesh: atoms: 32 (over y, x, core), grid: 4 (over z).
Axes of the slice: x: 4, y: 4, z: 4, core: 2. Of those that a mesh axis runs over, the one named last changes fastest.
Arguments:
- column_blocks: bfloat16 [1024, 32, 256], P('atoms'), may hold values from -1 to 1
- onsite: bfloat16 [1024, 256], P('atoms'), may hold values from -1 to 1
- neighbor_ids: int32 [1024, 32], P('atoms'), may hold values from 0 to 1023, as said below
- task_atoms: int32 [512, 32], P(('atoms', 'grid')), may hold values from 0 to 1023, as said below
- chem_shift: float32 [512], P(('atoms', 'grid')), may hold values from -0.6 to 0.6
- basis_values: bfloat16 [512, 512, 1024], P(('atoms', 'grid')), may hold values from -0.59765625 to 0.59765625
- box_start: int32 [512], P(('atoms', 'grid')), may hold values from 0 to 252
- box_row: int32 [512], P(('atoms', 'grid')), may hold values from 0 to 16
- box_col: int32 [512], P(('atoms', 'grid')), may hold values from 0 to 112
Outputs:
- density_cols: bfloat16 [512, 512, 128], P(('atoms', 'grid'))
- rho: float32 [256, 32, 128], P('grid')
Inputs may be any that keep to these rules, and one draw needn't show every extreme that they name: `task_atoms`: row a of a device's block of 4 tasks, task t, names 8 atoms from each of 4 devices' columns. The atoms named by one device's tasks are all different; at most 8 of them lie in one device's columns, and some device's columns hold exactly 8 of them. `neighbor_ids`: an atom's 32 entries are different atoms, never the atom itself.
All inputs are finite; a program needn't handle non-finite values. Where the computation divides by a largest or mean magnitude, that divisor is 1e-20 or more.
Results may differ from a plain program's by a relative error of at most 0.007.
Values may be sent and summed in bfloat16 or wider, within the bound.
A program may use at most 64 MiB of HBM per device.

v0:
```python
import math

import jax
import jax.numpy as jnp
from jax import lax
from jax.sharding import Mesh
from jax.sharding import PartitionSpec as P

BS = 16
KNB = 32
ITERS = 3
BOXP = 4
BOX_ROWS = 16
BOX_COLS = 16
GRID_ROWS = 32
GRID_COLS = 128
PL_SLAB = 64
CENTRAL = 128
ATOMS = ("atoms_0", "atoms_1", "atoms_2")
ATOMS_GRID = ("atoms_0", "atoms_1", "atoms_2", "grid")


exact_mode = lax.Precision.HIGHEST


def side_by_side(arrays, axis, dim, along):
    widths = [math.prod(a.shape[along:]) for a in arrays]
    both = jnp.concatenate(
        [a.reshape(*a.shape[:along], w) for a, w in zip(arrays, widths)], axis=along
    )
    out = lax.all_gather(both, axis, axis=dim, tiled=True)
    blocks = jnp.split(out, [sum(widths[:k]) for k in range(1, len(widths))], axis=along)
    return tuple((b.reshape(*out.shape[:along], *a.shape[along:]) for a, b in zip(arrays, blocks)))


def cut_along(value, dim, count):
    before, after = (value.shape[:dim], value.shape[dim + 1 :])
    return jnp.moveaxis(value.reshape(*before, count, -1, *after), dim, 0)


def sent_and_summed(value, axis, dim):
    blocks = cut_along(value, dim, lax.axis_size(axis))
    arrived = lax.all_to_all(blocks, axis, split_axis=0, concat_axis=0, tiled=True)
    return arrived.astype(jnp.float32).sum(axis=0)


def filled_up(lines, count):
    spare = -len(lines) % count
    return jnp.pad(lines, [(0, spare)] + [(0, 0)] * (lines.ndim - 1))


def from_everyone(value, axis):
    count = lax.axis_size(axis)
    return lax.all_to_all(
        jnp.broadcast_to(value[None], (count, *value.shape)), axis, 0, 0, tiled=True
    )


def in_order(blocks, dim):
    lengths = list(blocks.shape[1:])
    lengths[dim] *= blocks.shape[0]
    return jnp.moveaxis(blocks, 0, dim).reshape(lengths)


def gathered_by_axis(value, axes, dim):
    far, near = axes
    blocks = from_everyone(from_everyone(value, far), near)
    return in_order(blocks.swapaxes(0, 1).reshape(-1, *value.shape), dim)


def sum_in_two_steps(value, axes, dim):
    far, near = axes
    blocks = cut_along(value, dim, lax.axis_size(far))
    nearer = sent_and_summed(blocks, near, dim + 1)
    arrived = lax.all_to_all(
        nearer.astype(jnp.bfloat16), far, split_axis=0, concat_axis=0, tiled=True
    )
    return arrived.astype(jnp.float32).sum(axis=0)


def nested_sum(value, axes):
    lines = value.reshape(-1, value.shape[-1])
    padded = filled_up(lines, lax.axis_size(axes[0]) * lax.axis_size(axes[1]))
    whole = gathered_by_axis(sum_in_two_steps(padded, axes, 0).astype(jnp.bfloat16), axes, 0)
    return lax.slice_in_dim(whole, 0, len(lines)).reshape(value.shape).astype(jnp.float32)


def assemble(columns_in, onsite_in, links_in, members, offset):
    count = members.shape[0]
    matched = (links_in[None, :, :] == members[:, None, None]).astype(jnp.float32)
    blocks = columns_in.astype(jnp.float32).reshape(count, KNB, BS, BS)
    coupled = jnp.einsum("ijk,jkab->iajb", matched, blocks, precision=exact_mode)
    diagonal_part = jnp.einsum(
        "ij,jab->iajb",
        jnp.eye(count, dtype=jnp.float32),
        onsite_in.astype(jnp.float32).reshape(count, BS, BS),
        precision=exact_mode,
    )
    whole = (coupled + diagonal_part).reshape(count * BS, count * BS)
    return 0.5 * (whole + whole.T) - offset * jnp.eye(count * BS, dtype=jnp.float32)


def sign_columns(matrix):
    order_size = matrix.shape[0]
    identity = jnp.eye(order_size, dtype=jnp.float32)
    bound = jnp.max(jnp.sum(jnp.abs(matrix), axis=1)) + 1e-06
    iterate = (matrix / bound).astype(jnp.bfloat16)
    for iteration in range(ITERS - 1):
        squared = jnp.dot(iterate, iterate, preferred_element_type=jnp.float32)
        factor = (1.5 * identity - 0.5 * squared).astype(jnp.bfloat16)
        iterate = jnp.dot(iterate, factor, preferred_element_type=jnp.float32).astype(jnp.bfloat16)
    squared = jnp.dot(iterate, iterate[:, :CENTRAL], preferred_element_type=jnp.float32)
    factor = (1.5 * identity[:, :CENTRAL] - 0.5 * squared).astype(jnp.bfloat16)
    last_product = jnp.dot(iterate, factor, preferred_element_type=jnp.float32)
    return (0.5 * (identity[:, :CENTRAL] - last_product)).astype(jnp.bfloat16)


def collocate(density, basis_rows):
    weights = lax.dot_general(
        density, basis_rows, (((0,), (0,)), ((), ())), preferred_element_type=jnp.float32
    )
    values = jnp.sum(weights * basis_rows[:CENTRAL].astype(jnp.float32), axis=0)
    return values.reshape(BOXP, BOX_ROWS, BOX_COLS)


def on_device(
    column_blocks,
    onsite,
    neighbor_ids,
    task_atoms,
    chem_shift,
    basis_values,
    box_start,
    box_row,
    box_col,
):
    task_count, set_size = task_atoms.shape
    wanted_flat = task_atoms.reshape(-1)
    request_count = wanted_flat.shape[0]
    start_value = (
        jnp.zeros((request_count, KNB, BS * BS), jnp.bfloat16),
        jnp.zeros((request_count, BS * BS), jnp.bfloat16),
        jnp.zeros((request_count, KNB), jnp.int32),
    )
    blocks_piece, onsite_piece, links_piece = (
        *side_by_side((column_blocks, onsite), ATOMS, 0, 1),
        lax.all_gather(neighbor_ids, ATOMS, axis=0, tiled=True),
    )
    width_here = blocks_piece.shape[0]
    chosen = wanted_flat[:, None] == jnp.arange(width_here, dtype=jnp.int32)[None, :]
    chosen_half = chosen.astype(jnp.bfloat16)
    got_blocks = jnp.dot(
        chosen_half, blocks_piece.reshape(width_here, -1), preferred_element_type=jnp.float32
    )
    got_onsite = jnp.dot(chosen_half, onsite_piece, preferred_element_type=jnp.float32)
    got_links = jnp.dot(
        chosen.astype(jnp.float32), links_piece.astype(jnp.float32), precision=exact_mode
    )
    columns_in = got_blocks.astype(jnp.bfloat16).reshape(start_value[0].shape)
    onsite_in = got_onsite.astype(jnp.bfloat16)
    links_in = got_links.astype(jnp.int32)
    columns_in = columns_in.reshape(task_count, set_size, KNB, BS * BS)
    onsite_in = onsite_in.reshape(task_count, set_size, BS * BS)
    links_in = links_in.reshape(task_count, set_size, KNB)

    def one_task(members):
        block_cols, onsite_cols, link_cols, atom_ids, offset, basis_rows = members
        density = sign_columns(assemble(block_cols, onsite_cols, link_cols, atom_ids, offset))
        return (density, collocate(density, basis_rows))

    density_cols, boxes = lax.map(
        one_task, (columns_in, onsite_in, links_in, task_atoms, chem_shift, basis_values)
    )
    slab_count = lax.axis_size("grid")
    planes = PL_SLAB * slab_count

    def add_box(index, grid_now):
        corner = (box_start[index], box_row[index], box_col[index])
        current = lax.dynamic_slice(grid_now, corner, (BOXP, BOX_ROWS, BOX_COLS))
        return lax.dynamic_update_slice(grid_now, current + boxes[index], corner)

    partial_grid = lax.fori_loop(
        0, task_count, add_box, jnp.zeros((planes, GRID_ROWS, GRID_COLS), jnp.float32)
    )
    slab_piece = sent_and_summed(partial_grid.astype(jnp.bfloat16), "grid", 0)
    slab_values = nested_sum(slab_piece.astype(jnp.bfloat16), (("atoms_0", "atoms_1"), "atoms_2"))
    return (density_cols, slab_values)


def solution(mesh):
    torus = Mesh(
        mesh.devices.reshape(4, 4, 2, mesh.shape["grid"]), ("atoms_0", "atoms_1", "atoms_2", "grid")
    )
    return jax.shard_map(
        on_device,
        mesh=torus,
        in_specs=(
            P(ATOMS, None, None),
            P(ATOMS, None),
            P(ATOMS, None),
            P(ATOMS_GRID, None),
            P(ATOMS_GRID),
            P(ATOMS_GRID, None, None),
            P(ATOMS_GRID),
            P(ATOMS_GRID),
            P(ATOMS_GRID),
        ),
        out_specs=(P(ATOMS_GRID, None, None), P("grid", None, None)),
        check_vma=False,
    )
```

profile of v0, /device:TPU:1, one launch (start us, length us, event | category | flops | bytes accessed | tf_op | source)
XLA Modules:
  0.0 351.9 jit_solution(16138965034997109626)
XLA Ops:
  7.2 1.3 copy.46
  8.5 1.6 pad_maximum_fusion
  10.9 26.8 %all_gather.7 = s32[1024,32]{1,0:T(8,128)S(1)} all-gather(s32[32,32]{1,0:T(8,128)} %param.15), channel_id=1, replica_groups=mesh['atoms_0'=4,'atoms_1'=4,'atoms_2'=2,'grid'=4] {'atoms_0','atoms_1',..., dimensions={0}, use_global_device_ids=true | all-gather | bytes 135168 | tf_op jit(solution)/shard_map/all_gather | solution.py:147
  38.4 50.1 %all-gather.2.cloned.1.call-done = bf16[1024,8448]{1,0:T(8,128)(2,1)} async-done(((bf16[32,8448]{1,0:T(8,128)(2,1)}), bf16[1024,8448]{1,0:T(8,128)(2,1)}) %all-gather.2.cloned.1.call-update) | async-done | bytes 17301520 | tf_op jit(solution)/shard_map/all_gather | solution.py:31
  88.5 8.1 %fusion.47 = bf16[128,8192]{1,0:T(8,128)(2,1)S(1)} fusion(bf16[1024,8448]{1,0:T(8,128)(2,1)} %all-gather.2.cloned.1.call-done, s32[128]{0:T(128)S(1)} %eq.47), kind=kOutput, calls=%fused_computation.65 | convolution fusion | flops 2148663296 | bytes 18874880 | tf_op jit(solution)/shard_map/dot_general | solution.py:152
  97.3 1.3 convolution_convert_fusion.2
  98.6 129.8 %while.25 = (s32[]{:T(128)}, bf16[4,512,128]{2,1,0:T(8,128)(2,1)}, f32[4,4,16,16]{3,2,1,0:T(8,128)S(1)}, bf16[4,32,32,256]{3,2,1,0:T(8,128)(2,1)S(1)}, s32[4,32,...) while((s32[]{:T(128)}, bf16[4,512,128]{2,1,0:T(8,128)(2,1)}, ...), condition=%wide.region_4.5_spmd, body=%wide.region_0.4_spmd.sunk | while | flops 1369342976 | bytes 36034168 | solution.py:171
  101.7 2.6 add_bitcast_fusion.2
  104.4 9.0 %copy.57 = f32[32,16,32,16]{3,2,1,0:T(8,128)} copy(f32[32,16,32,16]{0,3,1,2:T(8,128)} %add_bitcast_fusion.2) | data formatting | bytes 2097152 | tf_op jit(solution)/shard_map/while/body/eval_jaxpr/add | solution.py:99
  113.4 7.6 %reshape.52 = f32[512,512]{1,0:T(8,128)S(1)} reshape(f32[32,16,32,16]{3,2,1,0:T(8,128)} %copy.57) | data formatting | bytes 2097152 | tf_op jit(solution)/shard_map/while/body/eval_jaxpr/reshape | solution.py:99
  123.5 2.3 convolution_convert_fusion.6
  125.7 2.3 convolution_convert_fusion.7
  128.1 1.4 bitcast_dynamic-update-slice_fusion.2
  129.5 1.6 fusion.87
  134.2 2.6 add_bitcast_fusion.2
  136.8 9.0 %copy.57 = f32[32,16,32,16]{3,2,1,0:T(8,128)} copy(f32[32,16,32,16]{0,3,1,2:T(8,128)} %add_bitcast_fusion.2) | data formatting | bytes 2097152 | tf_op jit(solution)/shard_map/while/body/eval_jaxpr/add | solution.py:99
  145.8 7.6 %reshape.52 = f32[512,512]{1,0:T(8,128)S(1)} reshape(f32[32,16,32,16]{3,2,1,0:T(8,128)} %copy.57) | data formatting | bytes 2097152 | tf_op jit(solution)/shard_map/while/body/eval_jaxpr/reshape | solution.py:99
  155.9 2.3 convolution_convert_fusion.6
  158.2 2.3 convolution_convert_fusion.7
  160.5 1.4 bitcast_dynamic-update-slice_fusion.2
  161.9 1.6 fusion.87
  166.6 2.6 add_bitcast_fusion.2
  169.2 9.0 %copy.57 = f32[32,16,32,16]{3,2,1,0:T(8,128)} copy(f32[32,16,32,16]{0,3,1,2:T(8,128)} %add_bitcast_fusion.2) | data formatting | bytes 2097152 | tf_op jit(solution)/shard_map/while/body/eval_jaxpr/add | solution.py:99
  178.2 7.6 %reshape.52 = f32[512,512]{1,0:T(8,128)S(1)} reshape(f32[32,16,32,16]{3,2,1,0:T(8,128)} %copy.57) | data formatting | bytes 2097152 | tf_op jit(solution)/shard_map/while/body/eval_jaxpr/reshape | solution.py:99
  188.3 2.3 convolution_convert_fusion.6
  190.6 2.3 convolution_convert_fusion.7
  192.9 1.4 bitcast_dynamic-update-slice_fusion.2
  194.3 1.6 fusion.87
  199.0 2.6 add_bitcast_fusion.2
  201.6 9.0 %copy.57 = f32[32,16,32,16]{3,2,1,0:T(8,128)} copy(f32[32,16,32,16]{0,3,1,2:T(8,128)} %add_bitcast_fusion.2) | data formatting | bytes 2097152 | tf_op jit(solution)/shard_map/while/body/eval_jaxpr/add | solution.py:99
  210.6 7.6 %reshape.52 = f32[512,512]{1,0:T(8,128)S(1)} reshape(f32[32,16,32,16]{3,2,1,0:T(8,128)} %copy.57) | data formatting | bytes 2097152 | tf_op jit(solution)/shard_map/while/body/eval_jaxpr/reshape | solution.py:99
  220.7 2.3 convolution_convert_fusion.6
  223.0 2.3 convolution_convert_fusion.7
  225.3 1.4 bitcast_dynamic-update-slice_fusion.2
  226.7 1.6 fusion.87
  228.4 2.5 broadcast_in_dim.34
  230.9 44.9 %while.26 = (s32[]{:T(128)}, f32[256,32,128]{2,1,0:T(8,128)}, s32[4]{0:T(128)S(1)}, s32[4]{0:T(128)S(1)}, s32[4]{0:T(128)S(1)}, /*index=5*/f32[4,4,16,16]{3,2,1,...) while((s32[]{:T(128)}, f32[256,32,128]{2,1,0:T(8,128)}, s32[4]{0:T(128)S(1)}, ...), condition=%wide.region_6.7_spmd, body=%wide.region_5.6_spmd.sunk | while | flops 1035 | bytes 20755 | solution.py:182
  239.4 2.7 dynamic_update_slice.22
  250.6 2.7 dynamic_update_slice.22
  261.8 2.7 dynamic_update_slice.22
  273.0 2.8 dynamic_update_slice.22
  275.8 2.7 convert_element_type.69
  278.5 29.4 %all_to_all.25 = bf16[4,64,32,128]{3,2,1,0:T(8,128)(2,1)S(1)} all-to-all(bf16[4,64,32,128]{3,2,1,0:T(8,128)(2,1)S(1)} %bitcast.121), channel_id=1, replica_groups=mesh['atoms_0'=4,'atoms_1'=4,'atoms_2'=2,'grid'=4] {'grid'}, dimensions={0} | all-to-all | bytes 4194304 | tf_op jit(solution)/shard_map/all_to_all | solution.py:43
  308.6 5.6 %all_to_all.26 = bf16[2,16,64,128]{3,2,1,0:T(8,128)(2,1)S(1)} all-to-all(bf16[2,16,64,128]{3,2,1,0:T(8,128)(2,1)S(1)} %copy.40), channel_id=1, replica_groups=mesh['atoms_0'=4,'atoms_1'=4,'atoms_2'=2,'grid'=4] {'atoms_2'}, dimensions={0} | all-to-all | bytes 1048576 | tf_op jit(solution)/shard_map/all_to_all | solution.py:43
  314.3 12.5 %all_to_all.27 = bf16[16,64,128]{2,1,0:T(8,128)(2,1)S(1)} all-to-all(bf16[16,64,128]{2,1,0:T(8,128)(2,1)S(1)} %reduce_sum.55), channel_id=1, replica_groups=mesh['atoms_0'=4,'atoms_1'=4,'atoms_2'=2,'grid'=4] {'atoms_0','atoms_1'}, dimensions={0} | all-to-all | bytes 524288 | tf_op jit(solution)/shard_map/all_to_all | solution.py:75
  326.9 10.4 %all_to_all.28 = bf16[16,64,128]{2,1,0:T(8,128)(2,1)S(1)} all-to-all(bf16[16,64,128]{2,1,0:T(8,128)(2,1)S(1)} %broadcast_in_dim.35), channel_id=1, replica_groups=mesh['atoms_0'=4,'atoms_1'=4,'atoms_2'=2,'grid'=4] {'atoms_0','atoms_1'}, dimensions={0} | all-to-all | bytes 524288 | tf_op jit(solution)/shard_map/all_to_all | solution.py:54
  337.4 6.5 %all_to_all.29 = bf16[2,16,64,128]{3,2,1,0:T(8,128)(2,1)S(1)} all-to-all(bf16[2,16,64,128]{3,2,1,0:T(8,128)(2,1)S(1)} %broadcast_in_dim.36), channel_id=1, replica_groups=mesh['atoms_0'=4,'atoms_1'=4,'atoms_2'=2,'grid'=4] {'atoms_2'}, dimensions={0} | all-to-all | bytes 1048576 | tf_op jit(solution)/shard_map/all_to_all | solution.py:54
  343.9 1.1 copy_convert_fusion
  (114 shorter events, 32.9 us)
Async XLA Ops:
  7.2 81.3 %all-gather.2.cloned.1.call-start = ((), (), s32[]{:S(2)}) async-start(), calls=%async_computation.5 | async-start | bytes 17842176 | tf_op jit(solution)/shard_map/all_gather | solution.py:31
  96.7 1.9 copy-start.2
  98.8 1.8 copy-start
  125.7 5.4 %copy-start.1 = (bf16[4,32,32,256]{3,2,1,0:T(8,128)(2,1)S(1)}, bf16[4,32,32,256]{3,2,1,0:T(8,128)(2,1)}, u32[]{:S(2)}) copy-start(bf16[4,32,32,256]{3,2,1,0:T(8,128)(2,1)} %copy-done) | copy-start | bytes 6291460 | tf_op jit(solution)/shard_map/while
  131.2 1.8 copy-start
  158.1 5.4 %copy-start.1 = (bf16[4,32,32,256]{3,2,1,0:T(8,128)(2,1)S(1)}, bf16[4,32,32,256]{3,2,1,0:T(8,128)(2,1)}, u32[]{:S(2)}) copy-start(bf16[4,32,32,256]{3,2,1,0:T(8,128)(2,1)} %copy-done) | copy-start | bytes 6291460 | tf_op jit(solution)/shard_map/while
  163.6 1.8 copy-start
  190.6 5.4 %copy-start.1 = (bf16[4,32,32,256]{3,2,1,0:T(8,128)(2,1)S(1)}, bf16[4,32,32,256]{3,2,1,0:T(8,128)(2,1)}, u32[]{:S(2)}) copy-start(bf16[4,32,32,256]{3,2,1,0:T(8,128)(2,1)} %copy-done) | copy-start | bytes 6291460 | tf_op jit(solution)/shard_map/while
  196.0 1.8 copy-start
  223.0 5.4 %copy-start.1 = (bf16[4,32,32,256]{3,2,1,0:T(8,128)(2,1)S(1)}, bf16[4,32,32,256]{3,2,1,0:T(8,128)(2,1)}, u32[]{:S(2)}) copy-start(bf16[4,32,32,256]{3,2,1,0:T(8,128)(2,1)} %copy-done) | copy-start | bytes 6291460 | tf_op jit(solution)/shard_map/while
  228.4 2.5 copy-start.3
  228.4 2.5 copy-start.4
  228.4 2.5 copy-start.5
Sparse Core Ops, SparseCore 0:
  10.8 77.6 all-gather.1
where the time goes:
time: 355 us; the launch traced here: 352 us
  local copies, waits for them, and re-layouts  103 us (29%)
  blocking collectives  91.2 us (26%)
  matrix products  51.2 us (14%)
  waiting for transfers between devices  50.1 us (14%)
  loops' own time  26.6 us (7%)
  other arithmetic  16 us (5%)
  between operations  14.2 us (4%)
    all_gather x1, waiting for transfers between devices, side_by_side(): out = lax.all_gather(both, axis, axis=dim, tiled=True)  50.1 us
    add x4, local copies, waits for them, and re-layouts, assemble(): whole = (coupled + diagonal_part).reshape(count * BS, count * BS)  35.9 us
    all_to_all x2, blocking collectives, sent_and_summed(): lax.all_to_all(blocks, axis, split_axis=0, concat_axis=0, tiled=True)  35 us
    reshape x8, local copies, waits for them, and re-layouts, assemble(): whole = (coupled + diagonal_part).reshape(count * BS, count * BS)  31.7 us
    all_gather x1, blocking collectives, on_device(): lax.all_gather(neighbor_ids, ATOMS, axis=0, tiled=True)  26.8 us
    another operation x1, loops' own time, on_device(): lax.fori_loop(0, task_count, add_box, jnp.zeros((planes, GRID_ROWS, GRID_...  23.3 us
    dot_general x8, matrix products, sign_columns(): jnp.dot(iterate, factor, preferred_element_type=jnp.float32)  18.5 us
    all_to_all x2, blocking collectives, from_everyone(): lax.all_to_all(jnp.broadcast_to(value[None], (count, *value.shape)), axis...  16.9 us
  transfers between devices with their start and end apart: 1, of which 1 were waited for; matrix products, arithmetic and copies ran while one was open for 0% of the time, Pallas kernels for 0%

commit v1 on v0

v1 whole, which is shorter than its diff:
```python
import jax, jax.numpy as jnp
from jax import lax
from jax.experimental import pallas as pl
from jax.experimental.pallas import tpu as pltpu
from jax.sharding import Mesh
from jax.sharding import PartitionSpec as P

F32, BF16, I32 = jnp.float32, jnp.bfloat16, jnp.int32
BS, KNB, NNB, ORDER, CENTRAL, POINTS, ITERS = 16, 32, 32, 512, 128, 1024, 3


def iota(shape, dim):
    return lax.broadcasted_iota(I32, shape, dim)


def fill_constants(perm, spread):
    rows, cols = iota((ORDER, ORDER), 0), iota((ORDER, ORDER), 1)
    hit = (rows // BS == cols % NNB) & (rows % BS == cols // NNB)
    perm[...] = hit.astype(F32).astype(BF16)
    point, lane = iota((POINTS, 128), 0), iota((POINTS, 128), 1)
    spread[...] = (lane == 64 * (point // 512) + point % 16).astype(F32).astype(BF16)


def task_density(atoms, shift, blocks, onsite, ids, perm, mixed, work):
    lane = iota((NNB, 128), 1)
    row32 = iota((NNB, 256), 0)
    for g in range(4):
        picks = []
        for jj in range(8):
            j = 8 * g + jj
            hit = (ids[j : j + 1, :] == atoms) & (lane // KNB == jj % 4)
            hit = hit.astype(F32)
            none = jnp.zeros((NNB, 128), F32)
            picks.append(jnp.concatenate([hit, none] if jj < 4 else [none, hit], axis=1))
        pick = jnp.concatenate(picks, axis=0).astype(BF16)
        found = jnp.dot(pick, blocks(g), preferred_element_type=F32)
        parts = []
        for jj in range(8):
            j = 8 * g + jj
            part = found[NNB * jj : NNB * (jj + 1)]
            parts.append(part + jnp.where(row32 == j, onsite[j : j + 1, :].astype(F32), 0.0))
        for half in range(2):
            tiles = [p[:, 128 * half : 128 * (half + 1)] for p in parts]
            for step in (1, 2, 4):
                low = (lane // (BS * step)) % 2 == 0
                fresh = list(tiles)
                for p in range(8):
                    if p & step:
                        continue
                    q = p + step
                    fresh[p] = jnp.where(low, tiles[p], pltpu.roll(tiles[q], BS * step, 1))
                    fresh[q] = jnp.where(low, pltpu.roll(tiles[p], 128 - BS * step, 1), tiles[q])
                tiles = fresh
            for a in range(8):
                mixed[pl.ds((8 * half + a) * NNB, NNB), pl.ds(128 * g, 128)] = tiles[a].astype(BF16)
    whole = jnp.dot(perm[...], mixed[...], preferred_element_type=F32)
    eye = (iota((ORDER, ORDER), 0) == iota((ORDER, ORDER), 1))
    matrix = 0.5 * (whole + whole.T) - jnp.where(eye, shift, 0.0)
    bound = jnp.max(jnp.sum(jnp.abs(matrix), axis=0, keepdims=True), axis=1, keepdims=True) + 1e-6
    work[...] = (matrix * (1.0 / bound)).astype(BF16)

    def step(_, carry):
        x = work[...]
        squared = jnp.dot(x, x, preferred_element_type=F32)
        diag = iota((ORDER, ORDER), 0) == iota((ORDER, ORDER), 1)
        factor = (jnp.where(diag, 1.5, 0.0) - 0.5 * squared).astype(BF16)
        work[...] = jnp.dot(x, factor, preferred_element_type=F32).astype(BF16)
        return carry

    lax.fori_loop(0, ITERS - 1, step, 0)
    x = work[...]
    narrow = iota((ORDER, CENTRAL), 0) == iota((ORDER, CENTRAL), 1)
    squared = jnp.dot(x, x[:, :CENTRAL], preferred_element_type=F32)
    factor = (jnp.where(narrow, 1.5, 0.0) - 0.5 * squared).astype(BF16)
    last = jnp.dot(x, factor, preferred_element_type=F32)
    return (0.5 * (jnp.where(narrow, 1.0, 0.0) - last)).astype(BF16)


def task_box(density, basis, spread):
    weights = lax.dot_general(density, basis[...], (((0,), (0,)), ((), ())), preferred_element_type=F32)
    values = jnp.sum(weights * basis[:CENTRAL].astype(F32), axis=0, keepdims=True)
    values = values.astype(BF16).astype(F32)
    rows, points = iota((32, POINTS), 0), iota((32, POINTS), 1)
    laid = jnp.where((points // 16) % 32 == rows, values, 0.0).astype(BF16)
    return jnp.dot(laid, spread[...], preferred_element_type=F32)


def compute_kernel(shift_ref, atoms_ref, blocks_ref, onsite_ref, hi_ref, lo_ref, basis_ref, dens_ref, box_ref, perm, spread, mixed, work, total):
    t = pl.program_id(0)

    @pl.when(t == 0)
    def _():
        fill_constants(perm, spread)
        total[...] = jnp.zeros_like(total)

    ids = hi_ref[...].astype(F32) * 32.0 + lo_ref[...].astype(F32)
    density = task_density(
        atoms_ref[0], shift_ref[t],
        lambda g: blocks_ref[pl.ds(8 * g, 8)].reshape(256, 256),
        onsite_ref, ids, perm, mixed, work)
    dens_ref[0] = density
    placed = task_box(density, basis_ref.at[0], spread)
    total[...] += pltpu.roll(placed, 16 * t, 1)

    @pl.when(t == pl.num_programs(0) - 1)
    def _():
        box_ref[...] = total[...].astype(BF16)


def compute(shift, atoms, blocks, onsite, hi, lo, basis):
    tasks = atoms.shape[0]
    return pl.pallas_call(
        compute_kernel,
        grid=(tasks,),
        out_shape=(
            jax.ShapeDtypeStruct((tasks, ORDER, CENTRAL), BF16),
            jax.ShapeDtypeStruct((32, 128), BF16),
        ),
        in_specs=[
            pl.BlockSpec(memory_space=pltpu.SMEM),
            pl.BlockSpec((1, NNB, 128), lambda t: (t, 0, 0)),
            pl.BlockSpec((NNB, KNB, 256), lambda t: (t, 0, 0)),
            pl.BlockSpec((NNB, 256), lambda t: (t, 0)),
            pl.BlockSpec((NNB, 128), lambda t: (t, 0)),
            pl.BlockSpec((NNB, 128), lambda t: (t, 0)),
            pl.BlockSpec((1, ORDER, POINTS), lambda t: (t, 0, 0)),
        ],
        out_specs=(
            pl.BlockSpec((1, ORDER, CENTRAL), lambda t: (t, 0, 0)),
            pl.BlockSpec((32, 128), lambda t: (0, 0)),
        ),
        scratch_shapes=[
            pltpu.VMEM((ORDER, ORDER), BF16),
            pltpu.VMEM((POINTS, 128), BF16),
            pltpu.VMEM((ORDER, ORDER), BF16),
            pltpu.VMEM((ORDER, ORDER), BF16),
            pltpu.VMEM((32, 128), F32),
        ],
        compiler_params=pltpu.CompilerParams(vmem_limit_bytes=50 << 20),
    )(shift, atoms, blocks, onsite, hi, lo, basis)


AXES = ("atoms_0", "atoms_1", "atoms_2", "grid")


def linear_place():
    y, x, c, z = (lax.axis_index(a) for a in AXES)
    return ((y * 4 + x) * 2 + c) * 4 + z


def place_of(p):
    return (p // 32, (p // 8) % 4, (p // 4) % 2, p % 4)


def share_kernel(box_ref, where_ref, boxes_ref, wheres_ref, send_a, recv_a, send_b, recv_b):
    me = linear_place()
    count = boxes_ref.shape[0]
    barrier = pltpu.get_barrier_semaphore()

    def greet(d, carry):
        pl.semaphore_signal(barrier, inc=1, device_id=place_of((me + d) % count), device_id_type=pl.DeviceIdType.MESH)
        return carry

    lax.fori_loop(1, count, greet, 0)
    pl.semaphore_wait(barrier, count - 1)

    def send(d, carry):
        peer = place_of((me + d) % count)
        pltpu.make_async_remote_copy(box_ref, boxes_ref.at[me], send_a, recv_a, device_id=peer, device_id_type=pl.DeviceIdType.MESH).start()
        pltpu.make_async_remote_copy(where_ref, wheres_ref.at[me], send_b, recv_b, device_id=peer, device_id_type=pl.DeviceIdType.MESH).start()
        return carry

    lax.fori_loop(1, count, send, 0)
    boxes_ref[me] = box_ref[...]
    wheres_ref[me] = where_ref[...]
    others = pl.ds(0, count - 1)
    for sem in (send_a, recv_a):
        pltpu.make_async_copy(boxes_ref.at[others], boxes_ref.at[others], sem).wait()
    for sem in (send_b, recv_b):
        pltpu.make_async_copy(wheres_ref.at[others], wheres_ref.at[others], sem).wait()


def share(box, where, count):
    vmem = pl.BlockSpec(memory_space=pltpu.VMEM)
    return pl.pallas_call(
        share_kernel,
        out_shape=(
            jax.ShapeDtypeStruct((count, *box.shape), box.dtype),
            jax.ShapeDtypeStruct((count, *where.shape), where.dtype),
        ),
        in_specs=[vmem, vmem],
        out_specs=(vmem, vmem),
        scratch_shapes=[pltpu.SemaphoreType.DMA] * 4,
        compiler_params=pltpu.CompilerParams(collective_id=1, has_side_effects=True),
    )(box, where)


def add_kernel(where_ref, boxes_ref, out_ref, picked, grid, sem):
    slab = lax.axis_index("grid")
    first = slab * 64 - 3
    count = boxes_ref.shape[0] * 4
    grid[...] = jnp.zeros_like(grid)

    def note(b, found):
        start = where_ref[b // 4, 0, b % 4] - first
        picked[found] = b
        return found + ((start >= 0) & (start < 67)).astype(I32)

    found = lax.fori_loop(0, count, note, 0, unroll=8)
    lane = iota((32, 128), 1)

    def add(n, carry):
        b = picked[n]
        who, t = b // 4, b % 4
        start = where_ref[who, 0, t] - first
        row = where_ref[who, 0, t + 4]
        col = where_ref[who, 0, t + 8]
        box = boxes_ref[who].astype(F32)
        inside = (lane >= col) & (lane < col + 16)
        for h in range(2):
            moved = pltpu.roll(box, (col + 128 - 64 * h - 16 * t) % 128, 1)
            moved = jnp.where(inside, moved, 0.0)
            for k in range(2):
                grid[start + 2 * h + k, pl.ds(row, 16), :] += moved[16 * k : 16 * (k + 1)]
        return carry

    lax.fori_loop(0, found, add, 0)
    copy = pltpu.make_async_copy(grid.at[pl.ds(3, 64)], out_ref, sem)
    copy.start()
    copy.wait()


def add_boxes(wheres, boxes):
    return pl.pallas_call(
        add_kernel,
        out_shape=jax.ShapeDtypeStruct((64, 32, 128), F32),
        in_specs=[pl.BlockSpec(memory_space=pltpu.SMEM), pl.BlockSpec(memory_space=pltpu.VMEM)],
        out_specs=pl.BlockSpec(memory_space=pl.ANY),
        scratch_shapes=[
            pltpu.SMEM((boxes.shape[0] * 4 + 1,), I32),
            pltpu.VMEM((70, 32, 128), F32),
            pltpu.SemaphoreType.DMA,
        ],
    )(wheres, boxes)


def on_device(column_blocks, onsite, neighbor_ids, task_atoms, chem_shift, basis_values, box_start, box_row, box_col):
    ids = jnp.tile(neighbor_ids, (1, 4))
    mine = jnp.concatenate(
        [column_blocks.reshape(32, -1), onsite, (ids // 32).astype(BF16), (ids % 32).astype(BF16)], axis=1
    )
    everyone = lax.all_gather(mine, AXES[:3], axis=0, tiled=True)
    chosen = task_atoms.reshape(-1)[:, None] == jnp.arange(everyone.shape[0], dtype=I32)[None, :]
    got = jnp.dot(chosen.astype(BF16), everyone, preferred_element_type=F32).astype(BF16)
    blocks = got[:, :8192].reshape(128, 32, 256)
    atoms = jnp.broadcast_to(task_atoms.astype(F32)[:, :, None], (*task_atoms.shape, 128))
    density, box = compute(chem_shift, atoms, blocks, got[:, 8192:8448], got[:, 8448:8576], got[:, 8576:], basis_values)
    where = jnp.concatenate([box_start, box_row, box_col])
    where = jnp.pad(where, (0, 128 - where.shape[0]))[None, :]
    boxes, wheres = share(box, where, 128)
    return density, add_boxes(wheres, boxes)


def solution(mesh):
    torus = Mesh(mesh.devices.reshape(4, 4, 2, mesh.shape["grid"]), AXES)
    atoms, both = P(AXES[:3]), P(AXES)
    return jax.shard_map(
        on_device,
        mesh=torus,
        in_specs=(atoms, atoms, atoms, both, both, both, both, both, both),
        out_specs=(both, P("grid")),
        check_vma=False,
    )
```

time: 355 us -> 172 us (0.48)
  local copies, waits for them, and re-layouts: 103 us -> 4.27 us
  blocking collectives: 91.2 us -> 0 us
  Pallas kernels: 0 us -> 64.5 us
  matrix products: 51.2 us -> 8.58 us
  waiting for transfers between devices: 50.1 us -> 77.9 us
  loops' own time: 26.6 us -> 0 us
  other arithmetic: 16 us -> 1.67 us
    pallas_call x0 -> x3, Pallas kernels: none -> 64.5 us  [the longest x1 28.2 us: share(): pl.pallas_call(share_kernel, out_shape=(jax.ShapeDtypeStruct((count, *box...]
    all_to_all x5 -> x0, blocking collectives: 64.4 us -> none  [the longest x2 35 us: sent_and_summed(): lax.all_to_all(blocks, axis, split_axis=0, concat_axis=0, tiled=True)]
    dot_general x23 -> x1, matrix products: 51.2 us -> 8.58 us  [on_device(): jnp.dot(chosen.astype(BF16), everyone, preferred_element_type=F32)]
    add x4 -> x0, local copies, waits for them, and re-layouts: 35.9 us -> none  [assemble(): whole = (coupled + diagonal_part).reshape(count * BS, count * BS)]
    reshape x8 -> x0, local copies, waits for them, and re-layouts: 31.7 us -> none  [assemble(): whole = (coupled + diagonal_part).reshape(count * BS, count * BS)]
    all_gather x1, waiting for transfers between devices: 50.1 us -> 77.9 us  [on_device(): everyone = lax.all_gather(mine, AXES[:3], axis=0, tiled=True)]
    all_gather x1 -> x0, blocking collectives: 26.8 us -> none  [on_device(): lax.all_gather(neighbor_ids, ATOMS, axis=0, tiled=True)]
    another operation x2 -> x0, loops' own time: 26.6 us -> none  [the longest x1 23.3 us: on_device(): lax.fori_loop(0, task_count, add_box, jnp.zeros((planes, GRID_ROWS, GRID_...]
where the time goes in v1:
time: 172 us; the launch traced here: 171 us
  waiting for transfers between devices  77.9 us (45%)
  Pallas kernels  64.5 us (38%)
  between operations  14.2 us (8%)
  matrix products  8.58 us (5%)
  local copies, waits for them, and re-layouts  4.27 us (2%)
    all_gather x1, waiting for transfers between devices, on_device(): everyone = lax.all_gather(mine, AXES[:3], axis=0, tiled=True)  77.9 us
    pallas_call x1, Pallas kernels, share(): pl.pallas_call(share_kernel, out_shape=(jax.ShapeDtypeStruct((count, *box...  28.2 us
    pallas_call x1, Pallas kernels, compute(): pl.pallas_call(compute_kernel, grid=(tasks,), out_shape=(jax.ShapeDtypeSt...  19.2 us
    pallas_call x1, Pallas kernels, add_boxes(): pl.pallas_call(add_kernel, out_shape=jax.ShapeDtypeStruct((64, 32, 128),...  17 us
    dot_general x1, matrix products, on_device(): jnp.dot(chosen.astype(BF16), everyone, preferred_element_type=F32)  8.58 us
  transfers between devices with their start and end apart: 1, of which 1 were waited for; matrix products, arithmetic and copies ran while one was open for 0% of the time, Pallas kernels for 0%

profile of v1, /device:TPU:1, one launch (start us, length us, event | category | flops | bytes accessed | tf_op | source)
XLA Modules:
  0.0 171.1 jit_solution(15973097563067353681)
XLA Ops:
  7.2 0.0 copy-start.2
  7.2 0.0 copy-start.5
  7.2 0.0 copy-start.4
  7.2 0.0 copy-start.3
  7.2 0.0 all-gather.2.cloned.1.call-start
  7.3 0.7 tile.4
  8.0 0.1 tile.10
  8.1 1.3 copy.11
  9.5 1.6 pad_maximum_fusion
  11.0 0.0 all-gather.2.cloned.1.call-update
  11.0 0.0 copy-done.2
  11.0 0.1 eq.17
  11.1 0.0 copy-done.5
  11.1 0.0 copy-done.4
  11.1 0.0 copy-done.3
  11.1 0.1 pad_add_fusion
  11.2 0.5 pad_bitcast_fusion.where_ref
  11.8 77.9 %all-gather.2.cloned.1.call-done = bf16[1024,8704]{1,0:T(8,128)(2,1)} async-done(((bf16[32,8704]{1,0:T(8,128)(2,1)}), bf16[1024,8704]{1,0:T(8,128)(2,1)}) %all-gather.2.cloned.1.call-update) | async-done | bytes 17825808 | tf_op jit(solution)/shard_map/all_gather | solution.py:252
  89.6 8.6 %convolution_convert_fusion = bf16[128,8704]{1,0:T(8,128)(2,1)S(1)} fusion(bf16[1024,8704]{1,0:T(8,128)(2,1)} %all-gather.2.cloned.1.call-done, s32[128]{0:T(128)S(1)} %eq.17), kind=kOutput, calls=%fused_computation | convolution fusion | flops 2282946560 | bytes 20054528 | tf_op jit(solution)/shard_map/dot_general | solution.py:254
  98.2 0.2 slice.16
  98.4 0.0 copy-start.1
  98.5 0.6 copy.12
  99.1 0.1 broadcast_in_dim.4.atoms_ref
  99.1 0.0 copy-done.1
  99.1 19.2 %shard_map.104 = (bf16[4,512,128]{2,1,0:T(8,128)(2,1)}, bf16[32,128]{1,0:T(8,128)(2,1)S(1)}) custom-call(f32[4]{0:T(128)S(1)} %copy-done.1, f32[4,32,128]{2,1,0:T(8,128)S(1)} %broadcast_in_dim.4.atoms_ref, bf16[128,32,256]{2,1,0:T(8,128)(2,1)S(1)} %bitcast.7, bf16[128,256]{1,0:T(8,128)(2,1)S(1)} %slice.17.onsite_ref, ...), custom_call_target="tpu_custom_call" | custom-call | tf_op jit(solution)/shard_map/pallas_call | solution.py:112
  118.4 0.0 copy-start
  118.4 0.6 copy-done
  119.0 28.2 %shard_map.105 = (bf16[128,32,128]{2,1,0:T(8,128)(2,1)}, s32[128,1,128]{2,1,0:T(1,128)}) custom-call(bf16[32,128]{1,0:T(8,128)(2,1)} %copy-done, s32[1,128]{1,0:T(1,128)} %pad_bitcast_fusion.where_ref), custom_call_target="tpu_custom_call" | custom-call | tf_op jit(solution)/shard_map/pallas_call | solution.py:185
  147.2 17.0 %shard_map.106 = f32[64,32,128]{2,1,0:T(8,128)} custom-call(s32[128,1,128]{2,1,0:T(1,128)} %get-tuple-element.8.where_ref, bf16[128,32,128]{2,1,0:T(8,128)(2,1)} %get-tuple-element.9.boxes_ref), custom_call_target="tpu_custom_call" | custom-call | tf_op jit(solution)/shard_map/pallas_call | solution.py:234
  (4 shorter events, 0.0 us)
Async XLA Ops:
  7.2 3.9 %copy-start.2 = (s32[4,32]{1,0:T(4,128)S(1)}, s32[4,32]{1,0:T(4,128)}, u32[]{:S(2)}) copy-start(s32[4,32]{1,0:T(4,128)} %param.12) | copy-start | bytes 1540
  7.2 4.0 %copy-start.5 = (s32[4]{0:T(128)S(1)}, s32[4]{0:T(128)}, u32[]{:S(2)}) copy-start(s32[4]{0:T(128)} %param.15) | copy-start | bytes 52
  7.2 4.0 %copy-start.4 = (s32[4]{0:T(128)S(1)}, s32[4]{0:T(128)}, u32[]{:S(2)}) copy-start(s32[4]{0:T(128)} %param.16) | copy-start | bytes 52
  7.2 3.9 %copy-start.3 = (s32[4]{0:T(128)S(1)}, s32[4]{0:T(128)}, u32[]{:S(2)}) copy-start(s32[4]{0:T(128)} %param.17) | copy-start | bytes 52
  7.2 82.4 %all-gather.2.cloned.1.call-start = ((), (), s32[]{:S(2)}) async-start(), calls=%async_computation | async-start | bytes 18382848 | tf_op jit(solution)/shard_map/all_gather | solution.py:252
  98.4 0.7 copy-start.1
  118.4 0.6 copy-start
Sparse Core Ops, SparseCore 0:
  11.2 78.4 all-gather.1

commit v2 on v1

--- a/solution.py
+++ b/solution.py
@@ -85,7 +85,7 @@
     return jnp.dot(laid, spread[...], preferred_element_type=F32)
 
 
-def compute_kernel(shift_ref, atoms_ref, blocks_ref, onsite_ref, hi_ref, lo_ref, basis_ref, dens_ref, box_ref, perm, spread, mixed, work, total):
+def compute_kernel(shift_ref, atoms_ref, got_ref, gots_ref, basis_ref, dens_ref, box_ref, perm, spread, mixed, work, total):
     t = pl.program_id(0)
 
     @pl.when(t == 0)
@@ -93,11 +93,21 @@
         fill_constants(perm, spread)
         total[...] = jnp.zeros_like(total)
 
-    ids = hi_ref[...].astype(F32) * 32.0 + lo_ref[...].astype(F32)
-    density = task_density(
-        atoms_ref[0], shift_ref[t],
-        lambda g: blocks_ref[pl.ds(8 * g, 8)].reshape(256, 256),
-        onsite_ref, ids, perm, mixed, work)
+    def small(h, c):
+        return jnp.concatenate([gots_ref[h, c, half, 0] for half in range(2)], axis=0)
+
+    def blocks(g):
+        half, first = g // 2, 8 * (g % 2)
+        tiles = [
+            jnp.concatenate([got_ref[h, c, half, 0, first + j] for c in range(2)], axis=1)
+            for j in range(8)
+            for h in range(2)
+        ]
+        return jnp.concatenate(tiles, axis=0)
+
+    onsite = jnp.concatenate([small(0, 0), small(0, 1)], axis=1)
+    ids = small(1, 0).astype(F32) * 32.0 + small(1, 1).astype(F32)
+    density = task_density(atoms_ref[0], shift_ref[t], blocks, onsite, ids, perm, mixed, work)
     dens_ref[0] = density
     placed = task_box(density, basis_ref.at[0], spread)
     total[...] += pltpu.roll(placed, 16 * t, 1)
@@ -107,7 +117,7 @@
         box_ref[...] = total[...].astype(BF16)
 
 
-def compute(shift, atoms, blocks, onsite, hi, lo, basis):
+def compute(shift, atoms, got, gots, basis):
     tasks = atoms.shape[0]
     return pl.pallas_call(
         compute_kernel,
@@ -119,10 +129,8 @@
         in_specs=[
             pl.BlockSpec(memory_space=pltpu.SMEM),
             pl.BlockSpec((1, NNB, 128), lambda t: (t, 0, 0)),
-            pl.BlockSpec((NNB, KNB, 256), lambda t: (t, 0, 0)),
-            pl.BlockSpec((NNB, 256), lambda t: (t, 0)),
-            pl.BlockSpec((NNB, 128), lambda t: (t, 0)),
-            pl.BlockSpec((NNB, 128), lambda t: (t, 0)),
+            pl.BlockSpec((2, 2, 2, 1, 16, 16, 128), lambda t: (0, 0, 0, t, 0, 0, 0)),
+            pl.BlockSpec((2, 2, 2, 1, 16, 128), lambda t: (0, 0, 0, t, 0, 0)),
             pl.BlockSpec((1, ORDER, POINTS), lambda t: (t, 0, 0)),
         ],
         out_specs=(
@@ -137,7 +145,7 @@
             pltpu.VMEM((32, 128), F32),
         ],
         compiler_params=pltpu.CompilerParams(vmem_limit_bytes=50 << 20),
-    )(shift, atoms, blocks, onsite, hi, lo, basis)
+    )(shift, atoms, got, gots, basis)
 
 
 AXES = ("atoms_0", "atoms_1", "atoms_2", "grid")
@@ -244,17 +252,232 @@
     )(wheres, boxes)
 
 
+MESH = pl.DeviceIdType.MESH
+
+
+def gather_kernel(blocks_ref, small_ref, atoms_ref, got_ref, gots_ref, held, flat, wants_v, wants_s, to_sib, to_z, rows_sib, rows_z,
+                  own_sem, sib_send, send_sem, recv_sem, want_send, want_recv, move_sem, z_send, z_recv, zs_send, zs_recv):
+    y, x, c, z = (lax.axis_index(a) for a in AXES)
+    h, o = z % 2, 1 - c
+    here = (y, x, c, z)
+    sibling = (y, x, o, z)
+    up, down = (z + 1) % 4, (z + 3) % 4
+    z_peers = [(y, x, c, up), (y, x, o, up), (y, x, c, down), (y, x, o, down)]
+
+    def ring(f, dp, dq):
+        if f == 0:
+            return ((y + dq) % 4, (x + dp) % 4, c, z)
+        return ((y + dp) % 4, (x + dq) % 4, c, z)
+
+    def unit(f, dp, dq, s):
+        place = ring(f, dp, dq)
+        return ((place[0] * 4 + place[1]) * 2 + s) * 2 + f
+
+    barrier = pltpu.get_barrier_semaphore()
+    peers = [ring(0, 1, 0), ring(0, 3, 0), ring(0, 0, 1), ring(0, 0, 3), sibling] + z_peers
+    for peer in peers:
+        pl.semaphore_signal(barrier, inc=1, device_id=peer, device_id_type=MESH)
+
+    half_k = pl.ds(pl.multiple_of(16 * h, 16), 16)
+    mine = pl.ds(pl.multiple_of(128 * c, 128), 128)
+    theirs = pl.ds(pl.multiple_of(128 * o, 128), 128)
+    for f in range(2):
+        u = unit(f, 0, 0, c)
+        pltpu.make_async_copy(blocks_ref.at[pl.ds(16 * f, 16), half_k, mine], held.at[u, pl.ds(0, 16)], own_sem.at[f]).start()
+        pltpu.make_async_copy(small_ref.at[2 * h + c, f], held.at[u, 16], own_sem.at[f]).start()
+    pl.semaphore_wait(barrier, len(peers))
+    for f in range(2):
+        u = unit(f, 0, 0, c)
+        pltpu.make_async_remote_copy(blocks_ref.at[pl.ds(16 * f, 16), half_k, theirs], held.at[u, pl.ds(0, 16)], sib_send, recv_sem.at[u], device_id=sibling, device_id_type=MESH).start()
+        pltpu.make_async_remote_copy(small_ref.at[2 * h + o, f], held.at[u, 16], sib_send, recv_sem.at[u], device_id=sibling, device_id_type=MESH).start()
+
+    def send(f, u, dp, dq):
+        pltpu.make_async_remote_copy(held.at[u], held.at[u], send_sem, recv_sem.at[u], device_id=ring(f, dp, dq), device_id_type=MESH).start()
+
+    def arrived(u):
+        pltpu.make_async_copy(held.at[u], held.at[u], recv_sem.at[u]).wait()
+
+    def near(f, u):
+        send(f, u, 1, 0)
+        send(f, u, 3, 0)
+
+    def far(f, u):
+        send(f, u, 0, 1)
+        send(f, u, 0, 3)
+
+    for f in range(2):
+        u = unit(f, 0, 0, c)
+        pltpu.make_async_copy(held.at[u], held.at[u], own_sem.at[f]).wait()
+        near(f, u)
+    for f in range(2):
+        u = unit(f, 0, 0, o)
+        arrived(u)
+        near(f, u)
+    want_to = [z_peers[2], z_peers[3], z_peers[0], z_peers[1], sibling]
+    for slot, peer in enumerate(want_to):
+        pltpu.make_async_remote_copy(atoms_ref, wants_v.at[slot], want_send, want_recv, device_id=peer, device_id_type=MESH).start()
+    for s in (c, o):
+        for f in range(2):
+            far(f, unit(f, 0, 0, s))
+
+    def take_near(first):
+        s = c if first else o
+        for f in range(2):
+            u = unit(f, 3, 0, s)
+            arrived(u)
+            if first:
+                send(f, u, 1, 0)
+            far(f, u)
+            u = unit(f, 1, 0, s)
+            arrived(u)
+            if not first:
+                send(f, u, 3, 0)
+            far(f, u)
+
+    def take_far(dp, first):
+        s = c if first else o
+        for f in range(2):
+            u = unit(f, dp, 3, s)
+            arrived(u)
+            if first:
+                send(f, u, 0, 1)
+            u = unit(f, dp, 1, s)
+            arrived(u)
+            if not first:
+                send(f, u, 0, 3)
+
+    take_near(True)
+    take_near(False)
+    take_far(0, True)
+    take_far(0, False)
+    for s in (c, o):
+        for f in range(2):
+            u = unit(f, 2, 0, s)
+            arrived(u)
+            far(f, u)
+    for dp in (3, 1, 2):
+        take_far(dp, True)
+        take_far(dp, False)
+    for dp in range(4):
+        for f in range(2):
+            for s in (c, o):
+                arrived(unit(f, dp, 2, s))
+
+    others = pl.ds(0, 5)
+    pltpu.make_async_copy(wants_v.at[others], wants_v.at[others], want_recv).wait()
+    moved = pltpu.make_async_copy(wants_v.at[others], wants_s.at[others], move_sem.at[0])
+    moved.start()
+    own = pltpu.make_async_copy(atoms_ref, wants_s.at[5], move_sem.at[1])
+    own.start()
+
+    for u in range(64):
+        flat[pl.ds(16 * u, 16), :] = held[u, 16].astype(F32)
+    moved.wait()
+    own.wait()
+
+    def pick(slot, t, j):
+        atom = wants_s[slot, t, j]
+        return held[atom // 16, atom % 16]
+
+    rows_f = pl.ds(0, 8)
+    for t in range(4):
+        for i in range(4):
+            base = 16 * (i // 2)
+
+            def one(r, carry, i=i, t=t, base=base):
+                to_z[i, 16 * t + r] = pick(i, t, base + r)
+                return carry
+
+            lax.fori_loop(0, 16, one, 0, unroll=16)
+            pltpu.make_async_remote_copy(to_z.at[i, pl.ds(16 * t, 16)], got_ref.at[h, c, pl.ds(64 * (i // 2) + 16 * t, 16)], z_send, z_recv.at[i, t], device_id=z_peers[i], device_id_type=MESH).start()
+    for half in range(2):
+        for t in range(4):
+            def two(r, carry, t=t, half=half):
+                at = 64 * half + 16 * t + r
+                to_sib[at] = pick(4, t, 16 * half + r)
+                got_ref[h, c, at] = pick(5, t, 16 * half + r)
+                return carry
+
+            lax.fori_loop(0, 16, two, 0, unroll=16)
+    pltpu.make_async_remote_copy(to_sib, got_ref.at[h, c], zs_send.at[0], z_recv.at[4, 0], device_id=sibling, device_id_type=MESH).start()
+
+    def line(slot, t, j):
+        atom = wants_s[slot, t, j]
+        return flat[pl.ds(atom, 1), :]
+
+    for i in range(4):
+        for t in range(4):
+            for_rows = [line(i, t, 16 * (i // 2) + r) for r in range(16)]
+            rows_z[i, pl.ds(16 * t, 16), :] = jnp.concatenate(for_rows, axis=0).astype(BF16)
+        pltpu.make_async_remote_copy(rows_z.at[i], gots_ref.at[h, c, pl.ds(64 * (i // 2), 64)], zs_send.at[1], zs_recv.at[i], device_id=z_peers[i], device_id_type=MESH).start()
+    for half in range(2):
+        for t in range(4):
+            at = pl.ds(64 * half + 16 * t, 16)
+            for_rows = [line(4, t, 16 * half + r) for r in range(16)]
+            rows_sib[at, :] = jnp.concatenate(for_rows, axis=0).astype(BF16)
+            for_rows = [line(5, t, 16 * half + r) for r in range(16)]
+            gots_ref[h, c, at, :] = jnp.concatenate(for_rows, axis=0).astype(BF16)
+    pltpu.make_async_remote_copy(rows_sib, gots_ref.at[h, c], zs_send.at[2], zs_recv.at[4], device_id=sibling, device_id_type=MESH).start()
+
+    def done(ref, sem):
+        pltpu.make_async_copy(ref, ref, sem).wait()
+
+    for i in range(4):
+        core = c if i % 2 == 0 else o
+        part = pl.ds(64 * (i // 2), 64)
+        for t in range(4):
+            done(got_ref.at[1 - h, core, pl.ds(64 * (i // 2) + 16 * t, 16)], z_recv.at[i, t])
+        done(gots_ref.at[1 - h, core, part], zs_recv.at[i])
+    done(got_ref.at[h, o], z_recv.at[4, 0])
+    done(gots_ref.at[h, o], zs_recv.at[4])
+    done(held.at[pl.ds(0, 2)], sib_send)
+    done(held.at[pl.ds(0, 60)], send_sem)
+    done(wants_v.at[others], want_send)
+    done(to_z, z_send)
+    done(to_sib, zs_send.at[0])
+    done(rows_z, zs_send.at[1])
+    done(rows_sib, zs_send.at[2])
+
+
+def gather(blocks, small, atoms):
+    any_space = pl.BlockSpec(memory_space=pl.ANY)
+    vmem = pl.BlockSpec(memory_space=pltpu.VMEM)
+    dma = pltpu.SemaphoreType.DMA
+    return pl.pallas_call(
+        gather_kernel,
+        out_shape=(
+            jax.ShapeDtypeStruct((2, 2, 128, 16, 128), BF16),
+            jax.ShapeDtypeStruct((2, 2, 128, 128), BF16),
+        ),
+        in_specs=[any_space, any_space, vmem],
+        out_specs=(vmem, vmem),
+        scratch_shapes=[
+            pltpu.VMEM((64, 17, 16, 128), BF16),
+            pltpu.VMEM((1024, 128), F32),
+            pltpu.VMEM((5, 4, 32), I32),
+            pltpu.SMEM((6, 4, 32), I32),
+            pltpu.VMEM((128, 16, 128), BF16),
+            pltpu.VMEM((4, 64, 16, 128), BF16),
+            pltpu.VMEM((128, 128), BF16),
+            pltpu.VMEM((4, 64, 128), BF16),
+            dma((2,)), dma, dma, dma((64,)), dma, dma, dma((2,)), dma, dma((5, 4)), dma((3,)), dma((5,)),
+        ],
+        compiler_params=pltpu.CompilerParams(collective_id=0, has_side_effects=True, vmem_limit_bytes=50 << 20),
+    )(blocks, small, atoms)
+
+
+def small_rows(onsite, neighbor_ids):
+    ids = jnp.tile(neighbor_ids, (1, 4))
+    pieces = jnp.stack([onsite[:, :128], onsite[:, 128:], (ids // 32).astype(BF16), (ids % 32).astype(BF16)])
+    return pieces.reshape(4, 2, 16, 128)
+
+
 def on_device(column_blocks, onsite, neighbor_ids, task_atoms, chem_shift, basis_values, box_start, box_row, box_col):
-    ids = jnp.tile(neighbor_ids, (1, 4))
-    mine = jnp.concatenate(
-        [column_blocks.reshape(32, -1), onsite, (ids // 32).astype(BF16), (ids % 32).astype(BF16)], axis=1
-    )
-    everyone = lax.all_gather(mine, AXES[:3], axis=0, tiled=True)
-    chosen = task_atoms.reshape(-1)[:, None] == jnp.arange(everyone.shape[0], dtype=I32)[None, :]
-    got = jnp.dot(chosen.astype(BF16), everyone, preferred_element_type=F32).astype(BF16)
-    blocks = got[:, :8192].reshape(128, 32, 256)
+    got, gots = gather(column_blocks, small_rows(onsite, neighbor_ids), task_atoms)
+    got = got.reshape(2, 2, 2, 4, 16, 16, 128)
+    gots = gots.reshape(2, 2, 2, 4, 16, 128)
     atoms = jnp.broadcast_to(task_atoms.astype(F32)[:, :, None], (*task_atoms.shape, 128))
-    density, box = compute(chem_shift, atoms, blocks, got[:, 8192:8448], got[:, 8448:8576], got[:, 8576:], basis_values)
+    density, box = compute(chem_shift, atoms, got, gots, basis_values)
     where = jnp.concatenate([box_start, box_row, box_col])
     where = jnp.pad(where, (0, 128 - where.shape[0]))[None, :]
     boxes, wheres = share(box, where, 128)

time: 172 us -> 119 us (0.69)
  waiting for transfers between devices: 77.9 us -> 0 us
  Pallas kernels: 64.5 us -> 111 us
  between operations: 14.2 us -> 0.71 us
  matrix products: 8.58 us -> 0 us
    all_gather x1 -> x0, waiting for transfers between devices: 77.9 us -> none  [on_device(): everyone = lax.all_gather(mine, AXES[:3], axis=0, tiled=True)]
    pallas_call x0 -> x1, Pallas kernels: none -> 48.5 us  [gather(): pl.pallas_call(gather_kernel, out_shape=(jax.ShapeDtypeStruct((2, 2, 128,...]
    dot_general x1 -> x0, matrix products: 8.58 us -> none  [on_device(): jnp.dot(chosen.astype(BF16), everyone, preferred_element_type=F32)]
  transfers between devices with their start and end apart: 1 -> 0, of which waited for: 1 -> 0; matrix products, arithmetic and copies ran while one was open for 0% -> 0% of each run, Pallas kernels for 0% -> 0%
where the time goes in v2:
time: 119 us; the launch traced here: 117 us
  Pallas kernels  111 us (93%)
  local copies, waits for them, and re-layouts  5.17 us (4%)
    pallas_call x1, Pallas kernels, gather(): pl.pallas_call(gather_kernel, out_shape=(jax.ShapeDtypeStruct((2, 2, 128,...  48.5 us
    pallas_call x1, Pallas kernels, share(): pl.pallas_call(share_kernel, out_shape=(jax.ShapeDtypeStruct((count, *box...  26.6 us
    pallas_call x1, Pallas kernels, compute(): pl.pallas_call(compute_kernel, grid=(tasks,), out_shape=(jax.ShapeDtypeSt...  19.3 us
    pallas_call x1, Pallas kernels, add_boxes(): pl.pallas_call(add_kernel, out_shape=jax.ShapeDtypeStruct((64, 32, 128),...  17 us
    unnamed x14, local copies, waits for them, and re-layouts  2.99 us

profile of v2, /device:TPU:1, one launch (start us, length us, event | category | flops | bytes accessed | tf_op | source)
XLA Modules:
  0.0 117.4 jit_solution(11638715165135998394)
XLA Ops:
  0.6 0.0 copy-start.6
  0.6 0.0 copy-start.5
  0.7 0.0 copy-start.4
  0.7 0.7 tile.4
  1.4 0.1 tile.10
  1.5 0.7 fusion.4
  2.3 0.0 copy-start
  2.3 1.0 copy-done
  3.3 0.0 copy-start.1
  3.3 0.7 copy-done.1
  4.0 48.5 %shard_map.104 = (bf16[2,2,128,16,128]{4,3,2,1,0:T(8,128)(2,1)S(1)}, bf16[2,2,128,128]{3,2,1,0:T(8,128)(2,1)S(1)}) custom-call(bf16[32,32,256]{2,1,0:T(8,128)(2,1)S(1)} %copy-done, bf16[4,2,16,128]{3,2,1,0:T(8,128)(2,1)S(1)} %pad_maximum_fusion.small_ref, s32[4,32]{1,0:T(4,128)S(1)} %copy-done.1), custom_call_target="tpu_custom_call" | custom-call | tf_op jit(solution)/shard_map/pallas_call | solution.py:446
  52.5 0.1 broadcast_in_dim.4.atoms_ref
  52.6 0.0 copy-start.3
  52.6 0.7 copy-done.3
  53.3 19.3 %shard_map.105 = (bf16[4,512,128]{2,1,0:T(8,128)(2,1)}, bf16[32,128]{1,0:T(8,128)(2,1)S(1)}) custom-call(f32[4]{0:T(128)S(1)} %copy-done.3, f32[4,32,128]{2,1,0:T(8,128)S(1)} %broadcast_in_dim.4.atoms_ref, bf16[2,2,2,4,16,16,128]{6,5,4,3,2,1,0:T(8,128)(2,1)S(1)} %bitcast.6, bf16[2,2,2,4,16,128]{5,4,3,2,1,0:T(8,128)(2,1)S(1)} %bitcast.7, ...), custom_call_target="tpu_custom_call" | custom-call | tf_op jit(solution)/shard_map/pallas_call | solution.py:122
  72.6 0.0 copy-start.2
  72.6 0.6 copy-done.2
  73.2 0.0 copy-done.6
  73.2 0.0 copy-done.5
  73.2 0.0 copy-done.4
  73.2 0.1 pad_add_fusion
  73.3 0.6 pad_bitcast_fusion.where_ref
  73.8 26.6 %shard_map.106 = (bf16[128,32,128]{2,1,0:T(8,128)(2,1)}, s32[128,1,128]{2,1,0:T(1,128)}) custom-call(bf16[32,128]{1,0:T(8,128)(2,1)} %copy-done.2, s32[1,128]{1,0:T(1,128)} %pad_bitcast_fusion.where_ref), custom_call_target="tpu_custom_call" | custom-call | tf_op jit(solution)/shard_map/pallas_call | solution.py:193
  100.5 17.0 %shard_map.107 = f32[64,32,128]{2,1,0:T(8,128)} custom-call(s32[128,1,128]{2,1,0:T(1,128)} %get-tuple-element.12.where_ref, bf16[128,32,128]{2,1,0:T(8,128)(2,1)} %get-tuple-element.13.boxes_ref), custom_call_target="tpu_custom_call" | custom-call | tf_op jit(solution)/shard_map/pallas_call | solution.py:242
  (3 shorter events, 0.0 us)
Async XLA Ops:
  0.6 72.6 %copy-start.6 = (s32[4]{0:T(128)S(1)}, s32[4]{0:T(128)}, u32[]{:S(2)}) copy-start(s32[4]{0:T(128)} %param.15) | copy-start | bytes 52
  0.6 72.6 %copy-start.5 = (s32[4]{0:T(128)S(1)}, s32[4]{0:T(128)}, u32[]{:S(2)}) copy-start(s32[4]{0:T(128)} %param.16) | copy-start | bytes 52
  0.7 72.6 %copy-start.4 = (s32[4]{0:T(128)S(1)}, s32[4]{0:T(128)}, u32[]{:S(2)}) copy-start(s32[4]{0:T(128)} %param.17) | copy-start | bytes 52
  2.3 1.0 copy-start
  3.3 0.7 copy-start.1
  52.6 0.7 copy-start.3
  72.6 0.6 copy-start.2

commit v3 on v2

v3 whole, which is shorter than its diff:
```python
import jax
import jax.numpy as jnp
from jax import lax
from jax.experimental import pallas as pl
from jax.experimental.pallas import tpu as pltpu
from jax.sharding import Mesh
from jax.sharding import PartitionSpec as P

F32, BF16, I32 = jnp.float32, jnp.bfloat16, jnp.int32
BS, KNB, NNB, ORDER, CENTRAL, POINTS, ITERS = 16, 32, 32, 512, 128, 1024, 3
SLAB, ROWS, COLS = 64, 32, 128
DEVICES, TASKS = 128, 4
AXES = ("atoms_0", "atoms_1", "atoms_2", "grid")
MESH = pl.DeviceIdType.MESH


def iota(shape, dim):
    return lax.broadcasted_iota(I32, shape, dim)


def fill_constants(perm):
    rows, cols = iota((ORDER, ORDER), 0), iota((ORDER, ORDER), 1)
    hit = (rows // BS == cols % NNB) & (rows % BS == cols // NNB)
    perm[...] = hit.astype(F32).astype(BF16)


def task_density(atoms, shift, blocks, onsite, ids, perm, mixed, work):
    lane = iota((NNB, 128), 1)
    row32 = iota((NNB, 256), 0)
    for g in range(4):
        picks = []
        for jj in range(8):
            j = 8 * g + jj
            hit = (ids[j : j + 1, :] == atoms) & (lane // KNB == jj % 4)
            hit = hit.astype(F32)
            none = jnp.zeros((NNB, 128), F32)
            picks.append(jnp.concatenate([hit, none] if jj < 4 else [none, hit], axis=1))
        pick = jnp.concatenate(picks, axis=0).astype(BF16)
        found = jnp.dot(pick, blocks(g), preferred_element_type=F32)
        parts = []
        for jj in range(8):
            j = 8 * g + jj
            part = found[NNB * jj : NNB * (jj + 1)]
            parts.append(part + jnp.where(row32 == j, onsite[j : j + 1, :].astype(F32), 0.0))
        for half in range(2):
            tiles = [p[:, 128 * half : 128 * (half + 1)] for p in parts]
            for step in (1, 2, 4):
                low = (lane // (BS * step)) % 2 == 0
                fresh = list(tiles)
                for p in range(8):
                    if p & step:
                        continue
                    q = p + step
                    fresh[p] = jnp.where(low, tiles[p], pltpu.roll(tiles[q], BS * step, 1))
                    fresh[q] = jnp.where(low, pltpu.roll(tiles[p], 128 - BS * step, 1), tiles[q])
                tiles = fresh
            for a in range(8):
                mixed[pl.ds((8 * half + a) * NNB, NNB), pl.ds(128 * g, 128)] = tiles[a].astype(BF16)
    whole = jnp.dot(perm[...], mixed[...], preferred_element_type=F32)
    eye = iota((ORDER, ORDER), 0) == iota((ORDER, ORDER), 1)
    matrix = 0.5 * (whole + whole.T) - jnp.where(eye, shift, 0.0)
    bound = jnp.max(jnp.sum(jnp.abs(matrix), axis=0, keepdims=True), axis=1, keepdims=True) + 1e-6
    work[...] = (matrix * (1.0 / bound)).astype(BF16)

    def step(_, carry):
        x = work[...]
        squared = jnp.dot(x, x, preferred_element_type=F32)
        diag = iota((ORDER, ORDER), 0) == iota((ORDER, ORDER), 1)
        factor = (jnp.where(diag, 1.5, 0.0) - 0.5 * squared).astype(BF16)
        work[...] = jnp.dot(x, factor, preferred_element_type=F32).astype(BF16)
        return carry

    lax.fori_loop(0, ITERS - 1, step, 0)
    x = work[...]
    narrow = iota((ORDER, CENTRAL), 0) == iota((ORDER, CENTRAL), 1)
    squared = jnp.dot(x, x[:, :CENTRAL], preferred_element_type=F32)
    factor = (jnp.where(narrow, 1.5, 0.0) - 0.5 * squared).astype(BF16)
    last = jnp.dot(x, factor, preferred_element_type=F32)
    return (0.5 * (jnp.where(narrow, 1.0, 0.0) - last)).astype(BF16)


def task_box(density, basis):
    weights = lax.dot_general(density, basis[...], (((0,), (0,)), ((), ())), preferred_element_type=F32)
    values = jnp.sum(weights * basis[:CENTRAL].astype(F32), axis=0, keepdims=True)
    box = jnp.concatenate([values[:, 128 * l : 128 * (l + 1)] for l in range(8)], axis=0)
    row, lane = iota((8, 128), 0), iota((8, 128), 1)
    for step in (1, 2, 4):
        high_row, high_lane = (row // step) % 2 == 1, (lane // (BS * step)) % 2 == 1
        from_below = pltpu.roll(pltpu.roll(box, 8 - step, 0), BS * step, 1)
        from_above = pltpu.roll(pltpu.roll(box, step, 0), 128 - BS * step, 1)
        crossed = jnp.where(high_row, from_above, from_below)
        box = jnp.where(high_row == high_lane, box, crossed)
    return box.astype(BF16)


def slab_list(wheres, first):
    rows = wheres[...].astype(F32)
    lane = iota((DEVICES, 128), 1)
    start = rows - first
    hit = ((start >= 0) & (start < SLAB + 3) & (lane < TASKS)).astype(F32)
    below = (iota((DEVICES, DEVICES), 1) < iota((DEVICES, DEVICES), 0)).astype(F32).astype(BF16)
    before = jnp.dot(below, hit.astype(BF16), preferred_element_type=F32)
    totals = jnp.sum(hit, axis=0, keepdims=True)
    turned = rows.T
    slots = iota((DEVICES, 512), 1).astype(F32)
    base = jnp.zeros((1, 1), F32)
    listed = jnp.zeros((8, 512), F32)
    line = iota((8, 128), 0)
    device = iota((8, 128), 1).astype(F32)
    for t in range(TASKS):
        chosen = (before[:, t : t + 1] + base == slots) & (hit[:, t : t + 1] > 0.5)
        values = jnp.where(line == 3, device, jnp.where(line == 4, float(t), 0.0))
        for v in range(3):
            values = jnp.where(line == v, turned[4 * v + t : 4 * v + t + 1, :], values)
        listed += jnp.dot(values.astype(BF16), chosen.astype(F32).astype(BF16), preferred_element_type=F32)
        base = base + totals[:, t : t + 1]
    row, slot = iota((8, 512), 0), iota((8, 512), 1).astype(F32)
    used = slot < base
    listed = jnp.where(row == 0, jnp.where(used, listed - first, SLAB + 6.0), listed)
    return jnp.where(row == 5, base, listed).astype(I32)


def main_kernel(blocks_ref, onsite_ref, ids_ref, atoms_ref, shift_ref, basis_ref, start_ref, row_ref, col_ref,
                dens_ref, boxes_ref, list_ref,
                held, flat, got, gots, to_sib, to_z, rows_f, rows_sib, rows_z, small, onsite_v, ids_v, atoms_v, basis_v,
                wants_v, wants_s, shift_s, where_s, where_v, wheres, own_box, perm, mixed, work,
                load_sem, basis_sem, own_sem, sib_send, send_sem, recv_sem, want_send, want_recv, move_sem, z_send, z_recv, zs_send, zs_recv,
                where_send, where_recv, box_send, box_recv):
    y, x, c, z = (lax.axis_index(a) for a in AXES)
    h, o = z % 2, 1 - c
    me = ((y * 4 + x) * 2 + c) * 4 + z
    sibling = (y, x, o, z)
    up, down = (z + 1) % 4, (z + 3) % 4
    z_peers = [(y, x, c, up), (y, x, o, up), (y, x, c, down), (y, x, o, down)]

    def ring(f, dp, dq):
        if f == 0:
            return ((y + dq) % 4, (x + dp) % 4, c, z)
        return ((y + dp) % 4, (x + dq) % 4, c, z)

    def unit(f, dp, dq, s):
        place = ring(f, dp, dq)
        return ((place[0] * 4 + place[1]) * 2 + s) * 2 + f

    def done(ref, sem):
        pltpu.make_async_copy(ref, ref, sem).wait()

    def for_others(act):
        def block(b, carry, skip=0):
            for d in range(skip, 8):
                act(((y + b // 4) % 4, (x + b % 4) % 4, (c + d // 4) % 2, (z + d % 4) % 4))
            return carry

        lax.fori_loop(1, 16, block, 0)
        block(0, 0, 1)

    barrier = pltpu.get_barrier_semaphore()
    for_others(lambda peer: pl.semaphore_signal(barrier, inc=1, device_id=peer, device_id_type=MESH))

    half_k = pl.ds(pl.multiple_of(16 * h, 16), 16)
    mine = pl.ds(pl.multiple_of(128 * c, 128), 128)
    theirs = pl.ds(pl.multiple_of(128 * o, 128), 128)
    loads = [
        pltpu.make_async_copy(onsite_ref, onsite_v, load_sem.at[0]),
        pltpu.make_async_copy(ids_ref, ids_v, load_sem.at[1]),
        pltpu.make_async_copy(atoms_ref, atoms_v, load_sem.at[2]),
        pltpu.make_async_copy(atoms_ref, wants_s.at[5], load_sem.at[3]),
        pltpu.make_async_copy(shift_ref, shift_s, load_sem.at[4]),
        pltpu.make_async_copy(start_ref, where_s.at[0], load_sem.at[5]),
        pltpu.make_async_copy(row_ref, where_s.at[1], load_sem.at[6]),
        pltpu.make_async_copy(col_ref, where_s.at[2], load_sem.at[7]),
    ]
    for load in loads:
        load.start()
    for f in range(2):
        u = unit(f, 0, 0, c)
        pltpu.make_async_copy(blocks_ref.at[pl.ds(16 * f, 16), half_k, mine], held.at[u, pl.ds(0, 16)], own_sem.at[f]).start()
    loads[0].wait()
    loads[1].wait()
    tiled = jnp.concatenate([ids_v[...]] * 4, axis=1)
    small[0] = onsite_v[:, :128].reshape(2, 16, 128)
    small[1] = onsite_v[:, 128:].reshape(2, 16, 128)
    small[2] = (tiled // 32).astype(F32).astype(BF16).reshape(2, 16, 128)
    small[3] = (tiled % 32).astype(F32).astype(BF16).reshape(2, 16, 128)
    for f in range(2):
        u = unit(f, 0, 0, c)
        pltpu.make_async_copy(small.at[2 * h + c, f], held.at[u, 16], own_sem.at[f]).start()
    pl.semaphore_wait(barrier, DEVICES - 1)
    for f in range(2):
        u = unit(f, 0, 0, c)
        pltpu.make_async_remote_copy(blocks_ref.at[pl.ds(16 * f, 16), half_k, theirs], held.at[u, pl.ds(0, 16)], sib_send, recv_sem.at[u], device_id=sibling, device_id_type=MESH).start()
        pltpu.make_async_remote_copy(small.at[2 * h + o, f], held.at[u, 16], sib_send, recv_sem.at[u], device_id=sibling, device_id_type=MESH).start()

    def send(f, u, dp, dq):
        pltpu.make_async_remote_copy(held.at[u], held.at[u], send_sem, recv_sem.at[u], device_id=ring(f, dp, dq), device_id_type=MESH).start()

    def arrived(u):
        done(held.at[u], recv_sem.at[u])

    def near(f, u):
        send(f, u, 1, 0)
        send(f, u, 3, 0)

    def far(f, u):
        send(f, u, 0, 1)
        send(f, u, 0, 3)

    for f in range(2):
        u = unit(f, 0, 0, c)
        done(held.at[u], own_sem.at[f])
        near(f, u)
    for f in range(2):
        u = unit(f, 0, 0, o)
        arrived(u)
        near(f, u)
    for s in (c, o):
        for f in range(2):
            far(f, unit(f, 0, 0, s))
    for load in loads[2:]:
        load.wait()
    for i in range(TASKS):
        pltpu.make_async_copy(basis_ref.at[i], basis_v.at[i], basis_sem.at[i]).start()
    want_to = [z_peers[2], z_peers[3], z_peers[0], z_peers[1], sibling]
    for slot, peer in enumerate(want_to):
        pltpu.make_async_remote_copy(atoms_v, wants_v.at[slot], want_send, want_recv, device_id=peer, device_id_type=MESH).start()
    lane1 = iota((1, 128), 1)
    where = jnp.zeros((1, 128), I32)
    for v in range(3):
        for t in range(TASKS):
            where = jnp.where(lane1 == 4 * v + t, where_s[v, t], where)
    where_v[...] = where
    wheres[pl.ds(me, 1), :] = where
    fill_constants(perm)

    def take_near(first):
        s = c if first else o
        for f in range(2):
            u = unit(f, 3, 0, s)
            arrived(u)
            if first:
                send(f, u, 1, 0)
            far(f, u)
            u = unit(f, 1, 0, s)
            arrived(u)
            if not first:
                send(f, u, 3, 0)
            far(f, u)

    def take_far(dp, first):
        s = c if first else o
        for f in range(2):
            u = unit(f, dp, 3, s)
            arrived(u)
            if first:
                send(f, u, 0, 1)
            u = unit(f, dp, 1, s)
            arrived(u)
            if not first:
                send(f, u, 0, 3)

    take_near(True)
    take_near(False)
    for_others(lambda peer: pltpu.make_async_remote_copy(where_v, wheres.at[pl.ds(me, 1)], where_send, where_recv, device_id=peer, device_id_type=MESH).start())
    take_far(0, True)
    take_far(0, False)
    for s in (c, o):
        for f in range(2):
            u = unit(f, 2, 0, s)
            arrived(u)
            far(f, u)
    for dp in (3, 1, 2):
        take_far(dp, True)
        take_far(dp, False)
    others = pl.ds(0, 5)
    done(wants_v.at[others], want_recv)
    moved = pltpu.make_async_copy(wants_v.at[others], wants_s.at[others], move_sem)
    moved.start()
    for dp in range(4):
        for f in range(2):
            for s in (c, o):
                arrived(unit(f, dp, 2, s))
    for u in range(64):
        flat[pl.ds(16 * u, 16), :] = held[u, 16].astype(F32)
    moved.wait()

    def pick(slot, t, j):
        atom = wants_s[slot, t, j]
        return held[atom // 16, atom % 16], flat[pl.ds(atom, 1), :]

    for t in range(TASKS):
        for i in range(4):
            part = i // 2

            def one(r, carry, i=i, t=t, part=part):
                to_z[i, 16 * t + r], rows_f[i, pl.ds(16 * t + r, 1), :] = pick(i, t, 16 * part + r)
                return carry

            lax.fori_loop(0, 16, one, 0, unroll=True)
            rows_z[i, pl.ds(16 * t, 16), :] = rows_f[i, pl.ds(16 * t, 16), :].astype(BF16)
            at = pl.ds(64 * part + 16 * t, 16)
            pltpu.make_async_remote_copy(to_z.at[i, pl.ds(16 * t, 16)], got.at[h, c, at], z_send, z_recv.at[i, t], device_id=z_peers[i], device_id_type=MESH).start()
            pltpu.make_async_remote_copy(rows_z.at[i, pl.ds(16 * t, 16)], gots.at[h, c, at], zs_send.at[1], zs_recv.at[i, t], device_id=z_peers[i], device_id_type=MESH).start()
    for t in range(TASKS):
        for part in range(2):
            first = 64 * part + 16 * t

            def two(r, carry, t=t, part=part, first=first):
                to_sib[first + r], rows_f[4, pl.ds(16 * part + r, 1), :] = pick(4, t, 16 * part + r)
                return carry

            def three(r, carry, t=t, part=part, first=first):
                got[h, c, first + r], rows_f[5, pl.ds(16 * part + r, 1), :] = pick(5, t, 16 * part + r)
                return carry

            lax.fori_loop(0, 16, two, 0, unroll=True)
            at = pl.ds(first, 16)
            rows_sib[at, :] = rows_f[4, pl.ds(16 * part, 16), :].astype(BF16)
            pltpu.make_async_remote_copy(to_sib.at[at], got.at[h, c, at], zs_send.at[0], z_recv.at[4, t], device_id=sibling, device_id_type=MESH).start()
            pltpu.make_async_remote_copy(rows_sib.at[at], gots.at[h, c, at], zs_send.at[2], zs_recv.at[4, t], device_id=sibling, device_id_type=MESH).start()
            lax.fori_loop(0, 16, three, 0, unroll=True)
            gots[h, c, at, :] = rows_f[5, pl.ds(16 * part, 16), :].astype(BF16)

    done(wheres.at[pl.ds(0, DEVICES - 1)], where_recv)
    list_ref[...] = slab_list(wheres, (z * SLAB - 3).astype(F32))

    def task(t, carry):
        for i in range(4):
            done(got.at[0, 0, pl.ds(0, 16)], z_recv.at[i, t])
            done(gots.at[0, 0, pl.ds(0, 16)], zs_recv.at[i, t])
        done(got.at[0, 0, pl.ds(0, 32)], z_recv.at[4, t])
        done(gots.at[0, 0, pl.ds(0, 32)], zs_recv.at[4, t])

        def rows(hh, cc):
            return jnp.concatenate([gots[hh, cc, pl.ds(pl.multiple_of(64 * part + 16 * t, 16), 16), :] for part in range(2)], axis=0)

        def blocks(g):
            first = 64 * (g // 2) + 16 * t + 8 * (g % 2)
            tiles = [
                jnp.concatenate([got[hh, cc, first + j] for cc in range(2)], axis=1)
                for j in range(8)
                for hh in range(2)
            ]
            return jnp.concatenate(tiles, axis=0)

        onsite = jnp.concatenate([rows(0, 0), rows(0, 1)], axis=1)
        ids = rows(1, 0).astype(F32) * 32.0 + rows(1, 1).astype(F32)
        eye = iota((NNB, NNB), 0) == iota((NNB, NNB), 1)
        atoms = jnp.sum(jnp.where(eye, atoms_v[pl.ds(t, 1), :].astype(F32), 0.0), axis=1, keepdims=True)
        density = task_density(atoms, shift_s[t], blocks, onsite, ids, perm, mixed, work)
        dens_ref[t] = density
        done(basis_v.at[0], basis_sem.at[t])
        box = task_box(density, basis_v.at[t])
        own_box[t] = box
        boxes_ref[me, t] = box
        for_others(lambda peer: pltpu.make_async_remote_copy(own_box.at[t], boxes_ref.at[me, t], box_send, box_recv.at[t], device_id=peer, device_id_type=MESH).start())
        return carry

    lax.fori_loop(0, TASKS, task, 0)
    for t in range(TASKS):
        done(boxes_ref.at[pl.ds(0, DEVICES - 1), t], box_recv.at[t])
    done(boxes_ref.at[pl.ds(0, DEVICES - 1)], box_send)
    done(held.at[pl.ds(0, 2)], sib_send)
    done(held.at[pl.ds(0, 60)], send_sem)
    done(wants_v.at[others], want_send)
    done(wheres.at[pl.ds(0, DEVICES - 1)], where_send)
    done(to_z, z_send)
    done(to_sib, zs_send.at[0])
    done(rows_z, zs_send.at[1])
    done(rows_sib, zs_send.at[2])


def run_main(*args):
    any_space = pl.BlockSpec(memory_space=pl.ANY)
    vmem = pl.BlockSpec(memory_space=pltpu.VMEM)
    dma = pltpu.SemaphoreType.DMA
    return pl.pallas_call(
        main_kernel,
        out_shape=(
            jax.ShapeDtypeStruct((TASKS, ORDER, CENTRAL), BF16),
            jax.ShapeDtypeStruct((DEVICES, TASKS, 8, 128), BF16),
            jax.ShapeDtypeStruct((8, 512), I32),
        ),
        in_specs=[any_space] * 9,
        out_specs=(vmem, vmem, vmem),
        scratch_shapes=[
            pltpu.VMEM((64, 17, 16, 128), BF16),
            pltpu.VMEM((1024, 128), F32),
            pltpu.VMEM((2, 2, 128, 16, 128), BF16),
            pltpu.VMEM((2, 2, 128, 128), BF16),
            pltpu.VMEM((128, 16, 128), BF16),
            pltpu.VMEM((4, 64, 16, 128), BF16),
            pltpu.VMEM((6, 64, 128), F32),
            pltpu.VMEM((128, 128), BF16),
            pltpu.VMEM((4, 64, 128), BF16),
            pltpu.VMEM((4, 2, 16, 128), BF16),
            pltpu.VMEM((32, 256), BF16),
            pltpu.VMEM((32, 32), I32),
            pltpu.VMEM((TASKS, NNB), I32),
            pltpu.VMEM((TASKS, ORDER, POINTS), BF16),
            pltpu.VMEM((5, TASKS, NNB), I32),
            pltpu.SMEM((6, TASKS, NNB), I32),
            pltpu.SMEM((TASKS,), F32),
            pltpu.SMEM((3, TASKS), I32),
            pltpu.VMEM((1, 128), I32),
            pltpu.VMEM((DEVICES, 128), I32),
            pltpu.VMEM((TASKS, 8, 128), BF16),
            pltpu.VMEM((ORDER, ORDER), BF16),
            pltpu.VMEM((ORDER, ORDER), BF16),
            pltpu.VMEM((ORDER, ORDER), BF16),
            dma((8,)), dma((TASKS,)), dma((2,)), dma, dma, dma((64,)), dma, dma, dma, dma, dma((5, TASKS)), dma((3,)), dma((5, TASKS)),
            dma, dma, dma, dma((TASKS,)),
        ],
        compiler_params=pltpu.CompilerParams(collective_id=0, has_side_effects=True, vmem_limit_bytes=56 << 20),
    )(*args)


def add_kernel(list_ref, boxes_ref, dens_ref, out_ref, dens_out, grid, sem, dens_sem):
    through = pltpu.make_async_copy(dens_ref, dens_out, dens_sem)
    through.start()
    grid[...] = jnp.zeros_like(grid)
    lane = iota((8, 128), 1)

    def add(n, carry):
        for m in range(4):
            at = 4 * n + m
            start, row, col = list_ref[0, at], list_ref[1, at], list_ref[2, at]
            box = boxes_ref[list_ref[3, at], list_ref[4, at]].astype(F32)
            inside = (lane >= col) & (lane < col + 16)
            for l in range(8):
                moved = jnp.where(inside, pltpu.roll(box, (col + 128 - 16 * l) % 128, 1), 0.0)
                grid[start + l // 2, pl.ds(row + 8 * (l % 2), 8), :] += moved
        return carry

    lax.fori_loop(0, (list_ref[5, 0] + 3) // 4, add, 0)
    copy = pltpu.make_async_copy(grid.at[pl.ds(3, SLAB)], out_ref, sem)
    copy.start()
    copy.wait()
    through.wait()


def add_boxes(listed, boxes, dens):
    any_space = pl.BlockSpec(memory_space=pl.ANY)
    vmem = pl.BlockSpec(memory_space=pltpu.VMEM)
    return pl.pallas_call(
        add_kernel,
        out_shape=(
            jax.ShapeDtypeStruct((SLAB, ROWS, COLS), F32),
            jax.ShapeDtypeStruct(dens.shape, dens.dtype),
        ),
        in_specs=[pl.BlockSpec(memory_space=pltpu.SMEM), vmem, vmem],
        out_specs=(any_space, any_space),
        scratch_shapes=[
            pltpu.VMEM((SLAB + 10, ROWS, COLS), F32),
            pltpu.SemaphoreType.DMA,
            pltpu.SemaphoreType.DMA,
        ],
    )(listed, boxes, dens)


def on_device(*args):
    dens, boxes, listed = run_main(*args)
    rho, dens = add_boxes(listed, boxes, dens)
    return dens, rho


def solution(mesh):
    torus = Mesh(mesh.devices.reshape(4, 4, 2, mesh.shape["grid"]), AXES)
    atoms, both = P(AXES[:3]), P(AXES)
    return jax.shard_map(
        on_device,
        mesh=torus,
        in_specs=(atoms, atoms, atoms, both, both, both, both, both, both),
        out_specs=(both, P("grid")),
        check_vma=False,
    )
```

time: 119 us -> 81.1 us (0.68); the launches traced: 117 us -> 81 us
  Pallas kernels: 111 us -> 80.3 us
  local copies, waits for them, and re-layouts: 5.17 us -> 0 us
    pallas_call x4 -> x2, Pallas kernels: 111 us -> 80.3 us  [the longest x1 72 us: run_main(): pl.pallas_call(main_kernel, out_shape=(jax.ShapeDtypeStruct((TASKS, ORDER...]
    unnamed x14 -> x0, local copies, waits for them, and re-layouts: 2.99 us -> none
where the time goes in v3:
time: 81.1 us; the launch traced here: 81 us
  Pallas kernels  80.3 us (99%)
    pallas_call x1, Pallas kernels, run_main(): pl.pallas_call(main_kernel, out_shape=(jax.ShapeDtypeStruct((TASKS, ORDER...  72 us
    pallas_call x1, Pallas kernels, add_boxes(): pl.pallas_call(add_kernel, out_shape=(jax.ShapeDtypeStruct((SLAB, ROWS, C...  8.29 us

profile of v3, /device:TPU:1, one launch (start us, length us, event | category | flops | bytes accessed | tf_op | source)
XLA Modules:
  0.0 81.0 jit_solution(6446167856810869791)
XLA Ops:
  0.6 72.0 %shard_map.104 = (bf16[4,512,128]{2,1,0:T(8,128)(2,1)}, bf16[128,4,8,128]{3,2,1,0:T(8,128)(2,1)}, s32[8,512]{1,0:T(8,128)}) custom-call(bf16[32,32,256]{2,1,0:T(8,128)(2,1)} %blocks_ref.1, bf16[32,256]{1,0:T(8,128)(2,1)} %onsite_ref.1, s32[32,32]{1,0:T(8,128)} %ids_ref.1, s32[4,32]{1,0:T(4,128)} %atoms_ref.1, f32[4]{0:T(128)} %shift_ref.1, ...), custom_call_target="tpu_custom_call" | custom-call | tf_op jit(solution)/shard_map/pallas_call | solution.py:376
  72.7 8.3 %shard_map.105 = (f32[64,32,128]{2,1,0:T(8,128)}, bf16[4,512,128]{2,1,0:T(8,128)(2,1)}) custom-call(s32[8,512]{1,0:T(8,128)} %get-tuple-element.7.list_ref, bf16[128,4,8,128]{3,2,1,0:T(8,128)(2,1)} %get-tuple-element.8.boxes_ref, bf16[4,512,128]{2,1,0:T(8,128)(2,1)} %get-tuple-element.9.dens_ref), custom_call_target="tpu_custom_call" | custom-call | tf_op jit(solution)/shard_map/pallas_call | solution.py:444

commit v4 on v3

--- a/solution.py
+++ b/solution.py
@@ -24,64 +24,138 @@
     perm[...] = hit.astype(F32).astype(BF16)
 
 
-def task_density(atoms, shift, blocks, onsite, ids, perm, mixed, work):
+def assemble(atoms_of, ids_of, onsite_of, tile_of, shift_of, perm, found, mixed, whole, pair, start):
+    keep = {}
     lane = iota((NNB, 128), 1)
-    row32 = iota((NNB, 256), 0)
-    for g in range(4):
+
+    def prepare():
+        keep["ids"], keep["onsite"], keep["atoms"] = ids_of(), onsite_of(), atoms_of()
+
+    def find(g):
         picks = []
         for jj in range(8):
             j = 8 * g + jj
-            hit = (ids[j : j + 1, :] == atoms) & (lane // KNB == jj % 4)
+            hit = (keep["ids"][j : j + 1, :] == keep["atoms"]) & (lane // KNB == jj % 4)
             hit = hit.astype(F32)
             none = jnp.zeros((NNB, 128), F32)
             picks.append(jnp.concatenate([hit, none] if jj < 4 else [none, hit], axis=1))
         pick = jnp.concatenate(picks, axis=0).astype(BF16)
-        found = jnp.dot(pick, blocks(g), preferred_element_type=F32)
-        parts = []
+        tiles = [jnp.concatenate([tile_of(8 * g + j, h, 0), tile_of(8 * g + j, h, 1)], axis=1) for j in range(8) for h in range(2)]
+        got = jnp.dot(pick, jnp.concatenate(tiles, axis=0), preferred_element_type=F32)
+        row = iota((8, 256), 0)
         for jj in range(8):
             j = 8 * g + jj
-            part = found[NNB * jj : NNB * (jj + 1)]
-            parts.append(part + jnp.where(row32 == j, onsite[j : j + 1, :].astype(F32), 0.0))
-        for half in range(2):
-            tiles = [p[:, 128 * half : 128 * (half + 1)] for p in parts]
-            for step in (1, 2, 4):
-                low = (lane // (BS * step)) % 2 == 0
-                fresh = list(tiles)
-                for p in range(8):
-                    if p & step:
-                        continue
-                    q = p + step
-                    fresh[p] = jnp.where(low, tiles[p], pltpu.roll(tiles[q], BS * step, 1))
-                    fresh[q] = jnp.where(low, pltpu.roll(tiles[p], 128 - BS * step, 1), tiles[q])
-                tiles = fresh
-            for a in range(8):
-                mixed[pl.ds((8 * half + a) * NNB, NNB), pl.ds(128 * g, 128)] = tiles[a].astype(BF16)
-    whole = jnp.dot(perm[...], mixed[...], preferred_element_type=F32)
-    eye = iota((ORDER, ORDER), 0) == iota((ORDER, ORDER), 1)
-    matrix = 0.5 * (whole + whole.T) - jnp.where(eye, shift, 0.0)
-    bound = jnp.max(jnp.sum(jnp.abs(matrix), axis=0, keepdims=True), axis=1, keepdims=True) + 1e-6
-    work[...] = (matrix * (1.0 / bound)).astype(BF16)
-
-    def step(_, carry):
-        x = work[...]
-        squared = jnp.dot(x, x, preferred_element_type=F32)
-        diag = iota((ORDER, ORDER), 0) == iota((ORDER, ORDER), 1)
-        factor = (jnp.where(diag, 1.5, 0.0) - 0.5 * squared).astype(BF16)
-        work[...] = jnp.dot(x, factor, preferred_element_type=F32).astype(BF16)
-        return carry
-
-    lax.fori_loop(0, ITERS - 1, step, 0)
-    x = work[...]
-    narrow = iota((ORDER, CENTRAL), 0) == iota((ORDER, CENTRAL), 1)
-    squared = jnp.dot(x, x[:, :CENTRAL], preferred_element_type=F32)
-    factor = (jnp.where(narrow, 1.5, 0.0) - 0.5 * squared).astype(BF16)
-    last = jnp.dot(x, factor, preferred_element_type=F32)
-    return (0.5 * (jnp.where(narrow, 1.0, 0.0) - last)).astype(BF16)
-
-
-def task_box(density, basis):
-    weights = lax.dot_general(density, basis[...], (((0,), (0,)), ((), ())), preferred_element_type=F32)
-    values = jnp.sum(weights * basis[:CENTRAL].astype(F32), axis=0, keepdims=True)
+            part = got[NNB * jj : NNB * (jj + 1)]
+            own = 8 * (j // 8)
+            line = part[own : own + 8] + jnp.where(row == j % 8, keep["onsite"][j : j + 1, :], 0.0)
+            pieces = [part[:own]] * (own > 0) + [line] + [part[own + 8 :]] * (own + 8 < NNB)
+            found[g, pl.ds(NNB * jj, NNB), :] = jnp.concatenate(pieces, axis=0).astype(BF16)
+
+    def turn(g, half):
+        block = lane // BS
+        tiles = []
+        for j in range(8):
+            tile = found[g, pl.ds(NNB * j, NNB), pl.ds(128 * half, 128)]
+            tiles.append(pltpu.roll(tile, BS * j, 1) if j else tile)
+        tiles = [tiles[-q % 8] for q in range(8)]
+        for step in (1, 2, 4):
+            odd = (block // step) % 2 == 1
+            tiles = [jnp.where(odd, tiles[(q - step) % 8], tiles[q]) for q in range(8)]
+        for a in range(8):
+            tile = pltpu.roll(tiles[a], 128 - BS * a, 1) if a else tiles[a]
+            mixed[pl.ds((8 * half + a) * NNB, NNB), pl.ds(128 * g, 128)] = tile
+
+    def order():
+        whole[...] = jnp.dot(perm[...], mixed[...], preferred_element_type=F32).astype(BF16)
+
+    def fold(r):
+        rows = pl.ds(128 * r, 128)
+        twice = whole[rows, :].astype(F32) + whole[:, rows].T.astype(F32)
+        eye = iota((128, 128), 0) == iota((128, 128), 1)
+        low, high = 128 * r, 128 * (r + 1)
+        diagonal = twice[:, low:high] - jnp.where(eye, 2.0 * shift_of(), 0.0)
+        pieces = [twice[:, :low]] * (r > 0) + [diagonal] + [twice[:, high:]] * (r < 3)
+        twice = jnp.concatenate(pieces, axis=1)
+        pair[rows, :] = twice
+        part = jnp.sum(jnp.abs(twice).reshape(16, 8, ORDER), axis=0)
+        keep["sum"] = part if r == 0 else keep["sum"] + part
+
+    def limit():
+        sums = jnp.sum(keep["sum"], axis=0, keepdims=True)
+        bound = 0.5 * jnp.max(sums, axis=1, keepdims=True) + 1e-6
+        keep["scale"] = 0.5 / bound
+
+    def scale(r):
+        rows = pl.ds(128 * r, 128)
+        start[rows, :] = (pair[rows, :] * keep["scale"]).astype(BF16)
+
+    steps = [prepare]
+    for g in range(4):
+        steps += [lambda g=g: find(g)] + [lambda g=g, half=half: turn(g, half) for half in range(2)]
+    steps += [order]
+    steps += [lambda r=r: fold(r) for r in range(4)] + [limit]
+    return steps, [lambda r=r: scale(r) for r in range(4)]
+
+
+def less_half(product, first):
+    pieces = []
+    width = product.shape[1]
+    for r in range(ORDER // 128):
+        rows = product[128 * r : 128 * (r + 1)]
+        lead = 128 * r - first
+        if 0 <= lead < width:
+            eye = iota((128, 128), 0) == iota((128, 128), 1)
+            cut = jnp.where(eye, 1.5, 0.0) - 0.5 * rows[:, lead : lead + 128]
+            parts = [-0.5 * rows[:, :lead]] * (lead > 0) + [cut] + [-0.5 * rows[:, lead + 128 :]] * (lead + 128 < width)
+            pieces.append(jnp.concatenate(parts, axis=1))
+        else:
+            pieces.append(-0.5 * rows)
+    return jnp.concatenate(pieces, axis=0).astype(BF16)
+
+
+def iterate(start, middle, late, factor, narrow, set_density, basis_of, set_box):
+    keep = {}
+
+    def square(source):
+        factor[...] = less_half(jnp.dot(source[...], source[...], preferred_element_type=F32), 0)
+
+    def multiply(source, target):
+        target[...] = jnp.dot(source[...], factor[...], preferred_element_type=F32).astype(BF16)
+
+    def last_factor():
+        narrow[...] = less_half(jnp.dot(late[...], late[:, :CENTRAL], preferred_element_type=F32), 0)
+
+    def last_product():
+        last = jnp.dot(late[...], narrow[...], preferred_element_type=F32)
+        eye = iota((CENTRAL, CENTRAL), 0) == iota((CENTRAL, CENTRAL), 1)
+        top = 0.5 * (jnp.where(eye, 1.0, 0.0) - last[:CENTRAL])
+        density = jnp.concatenate([top, 0.5 * (0.0 - last[CENTRAL:])], axis=0).astype(BF16)
+        set_density(density)
+        keep["density"] = density.T
+
+    def collocate(n):
+        basis = basis_of()
+        cols = pl.ds(512 * n, 512)
+        weights = jnp.dot(keep["density"], basis[:, cols], preferred_element_type=F32)
+        part = jnp.sum(weights * basis[:CENTRAL, cols].astype(F32), axis=0, keepdims=True)
+        keep.setdefault("values", []).append(part)
+
+    def finish():
+        set_box(pack_box(jnp.concatenate(keep["values"], axis=1)))
+
+    early = [lambda: square(start), lambda: multiply(start, middle)]
+    rest = [lambda: square(middle), lambda: multiply(middle, late), last_factor, last_product]
+    rest += [lambda n=n: collocate(n) for n in range(2)] + [finish]
+    return early, rest
+
+
+def interleaved(first, second):
+    marks = [((k + 0.5) / len(first), 0, k) for k in range(len(first))] + [((k + 0.5) / len(second), 1, k) for k in range(len(second))]
+    for _, which, k in sorted(marks):
+        (first, second)[which][k]()
+
+
+def pack_box(values):
     box = jnp.concatenate([values[:, 128 * l : 128 * (l + 1)] for l in range(8)], axis=0)
     row, lane = iota((8, 128), 0), iota((8, 128), 1)
     for step in (1, 2, 4):
@@ -123,12 +197,12 @@
 def main_kernel(blocks_ref, onsite_ref, ids_ref, atoms_ref, shift_ref, basis_ref, start_ref, row_ref, col_ref,
                 dens_ref, boxes_ref, list_ref,
                 held, flat, got, gots, to_sib, to_z, rows_f, rows_sib, rows_z, small, onsite_v, ids_v, atoms_v, basis_v,
-                wants_v, wants_s, shift_s, where_s, where_v, wheres, own_box, perm, mixed, work,
+                wants_v, wants_s, shift_s, where_s, where_v, wheres, own_box, perm, found, mixed, whole, pair, start, middle, late, factor, narrow,
                 load_sem, basis_sem, own_sem, sib_send, send_sem, recv_sem, want_send, want_recv, move_sem, z_send, z_recv, zs_send, zs_recv,
-                where_send, where_recv, box_send, box_recv):
+                where_send, where_recv, over_send, over_recv, box_send, box_recv, pass_send, pass_recv):
     y, x, c, z = (lax.axis_index(a) for a in AXES)
     h, o = z % 2, 1 - c
-    me = ((y * 4 + x) * 2 + c) * 4 + z
+    slot = c * 64 + (y * 4 + x) * 4 + z
     sibling = (y, x, o, z)
     up, down = (z + 1) % 4, (z + 3) % 4
     z_peers = [(y, x, c, up), (y, x, o, up), (y, x, c, down), (y, x, o, down)]
@@ -145,9 +219,9 @@
     def done(ref, sem):
         pltpu.make_async_copy(ref, ref, sem).wait()
 
-    def for_others(act):
+    def for_others(act, cores=1):
         def block(b, carry, skip=0):
-            for d in range(skip, 8):
+            for d in range(skip, 4 * cores):
                 act(((y + b // 4) % 4, (x + b % 4) % 4, (c + d // 4) % 2, (z + d % 4) % 4))
             return carry
 
@@ -155,7 +229,7 @@
         block(0, 0, 1)
 
     barrier = pltpu.get_barrier_semaphore()
-    for_others(lambda peer: pl.semaphore_signal(barrier, inc=1, device_id=peer, device_id_type=MESH))
+    for_others(lambda peer: pl.semaphore_signal(barrier, inc=1, device_id=peer, device_id_type=MESH), 2)
 
     half_k = pl.ds(pl.multiple_of(16 * h, 16), 16)
     mine = pl.ds(pl.multiple_of(128 * c, 128), 128)
@@ -164,17 +238,16 @@
         pltpu.make_async_copy(onsite_ref, onsite_v, load_sem.at[0]),
         pltpu.make_async_copy(ids_ref, ids_v, load_sem.at[1]),
         pltpu.make_async_copy(atoms_ref, atoms_v, load_sem.at[2]),
-        pltpu.make_async_copy(atoms_ref, wants_s.at[5], load_sem.at[3]),
-        pltpu.make_async_copy(shift_ref, shift_s, load_sem.at[4]),
-        pltpu.make_async_copy(start_ref, where_s.at[0], load_sem.at[5]),
-        pltpu.make_async_copy(row_ref, where_s.at[1], load_sem.at[6]),
-        pltpu.make_async_copy(col_ref, where_s.at[2], load_sem.at[7]),
+        pltpu.make_async_copy(shift_ref, shift_s, load_sem.at[3]),
+        pltpu.make_async_copy(start_ref, where_s.at[0], load_sem.at[4]),
+        pltpu.make_async_copy(row_ref, where_s.at[1], load_sem.at[5]),
+        pltpu.make_async_copy(col_ref, where_s.at[2], load_sem.at[6]),
     ]
     for load in loads:
         load.start()
     for f in range(2):
         u = unit(f, 0, 0, c)
-        pltpu.make_async_copy(blocks_ref.at[pl.ds(16 * f, 16), half_k, mine], held.at[u, pl.ds(0, 16)], own_sem.at[f]).start()
+        pltpu.make_async_copy(blocks_ref.at[pl.ds(16 * f, 16), half_k, mine], held.at[pl.ds(17 * u, 16)], own_sem.at[f]).start()
     loads[0].wait()
     loads[1].wait()
     tiled = jnp.concatenate([ids_v[...]] * 4, axis=1)
@@ -184,18 +257,18 @@
     small[3] = (tiled % 32).astype(F32).astype(BF16).reshape(2, 16, 128)
     for f in range(2):
         u = unit(f, 0, 0, c)
-        pltpu.make_async_copy(small.at[2 * h + c, f], held.at[u, 16], own_sem.at[f]).start()
+        pltpu.make_async_copy(small.at[2 * h + c, f], held.at[17 * u + 16], own_sem.at[f]).start()
     pl.semaphore_wait(barrier, DEVICES - 1)
     for f in range(2):
         u = unit(f, 0, 0, c)
-        pltpu.make_async_remote_copy(blocks_ref.at[pl.ds(16 * f, 16), half_k, theirs], held.at[u, pl.ds(0, 16)], sib_send, recv_sem.at[u], device_id=sibling, device_id_type=MESH).start()
-        pltpu.make_async_remote_copy(small.at[2 * h + o, f], held.at[u, 16], sib_send, recv_sem.at[u], device_id=sibling, device_id_type=MESH).start()
+        pltpu.make_async_remote_copy(blocks_ref.at[pl.ds(16 * f, 16), half_k, theirs], held.at[pl.ds(17 * u, 16)], sib_send, recv_sem.at[u], device_id=sibling, device_id_type=MESH).start()
+        pltpu.make_async_remote_copy(small.at[2 * h + o, f], held.at[17 * u + 16], sib_send, recv_sem.at[u], device_id=sibling, device_id_type=MESH).start()
 
     def send(f, u, dp, dq):
-        pltpu.make_async_remote_copy(held.at[u], held.at[u], send_sem, recv_sem.at[u], device_id=ring(f, dp, dq), device_id_type=MESH).start()
+        pltpu.make_async_remote_copy(held.at[pl.ds(17 * u, 17)], held.at[pl.ds(17 * u, 17)], send_sem, recv_sem.at[u], device_id=ring(f, dp, dq), device_id_type=MESH).start()
 
     def arrived(u):
-        done(held.at[u], recv_sem.at[u])
+        done(held.at[pl.ds(17 * u, 17)], recv_sem.at[u])
 
     def near(f, u):
         send(f, u, 1, 0)
@@ -207,7 +280,7 @@
 
     for f in range(2):
         u = unit(f, 0, 0, c)
-        done(held.at[u], own_sem.at[f])
+        done(held.at[pl.ds(17 * u, 17)], own_sem.at[f])
         near(f, u)
     for f in range(2):
         u = unit(f, 0, 0, o)
@@ -220,17 +293,18 @@
         load.wait()
     for i in range(TASKS):
         pltpu.make_async_copy(basis_ref.at[i], basis_v.at[i], basis_sem.at[i]).start()
+    atoms = atoms_v[...]
+    wants_v[5] = jnp.concatenate([atoms, atoms + lax.shift_right_logical(atoms, 4)], axis=1)
     want_to = [z_peers[2], z_peers[3], z_peers[0], z_peers[1], sibling]
-    for slot, peer in enumerate(want_to):
-        pltpu.make_async_remote_copy(atoms_v, wants_v.at[slot], want_send, want_recv, device_id=peer, device_id_type=MESH).start()
+    for slot_to, peer in enumerate(want_to):
+        pltpu.make_async_remote_copy(wants_v.at[5], wants_v.at[slot_to], want_send, want_recv, device_id=peer, device_id_type=MESH).start()
     lane1 = iota((1, 128), 1)
     where = jnp.zeros((1, 128), I32)
     for v in range(3):
         for t in range(TASKS):
             where = jnp.where(lane1 == 4 * v + t, where_s[v, t], where)
     where_v[...] = where
-    wheres[pl.ds(me, 1), :] = where
-    fill_constants(perm)
+    wheres[pl.ds(slot, 1), :] = where
 
     def take_near(first):
         s = c if first else o
@@ -260,7 +334,6 @@
 
     take_near(True)
     take_near(False)
-    for_others(lambda peer: pltpu.make_async_remote_copy(where_v, wheres.at[pl.ds(me, 1)], where_send, where_recv, device_id=peer, device_id_type=MESH).start())
     take_far(0, True)
     take_far(0, False)
     for s in (c, o):
@@ -271,21 +344,21 @@
     for dp in (3, 1, 2):
         take_far(dp, True)
         take_far(dp, False)
+    for_others(lambda peer: pltpu.make_async_remote_copy(where_v, wheres.at[pl.ds(slot, 1)], where_send, where_recv, device_id=peer, device_id_type=MESH).start())
     others = pl.ds(0, 5)
     done(wants_v.at[others], want_recv)
-    moved = pltpu.make_async_copy(wants_v.at[others], wants_s.at[others], move_sem)
+    moved = pltpu.make_async_copy(wants_v, wants_s, move_sem)
     moved.start()
     for dp in range(4):
         for f in range(2):
             for s in (c, o):
                 arrived(unit(f, dp, 2, s))
     for u in range(64):
-        flat[pl.ds(16 * u, 16), :] = held[u, 16].astype(F32)
+        flat[pl.ds(16 * u, 16), :] = held[17 * u + 16].astype(F32)
     moved.wait()
 
     def pick(slot, t, j):
-        atom = wants_s[slot, t, j]
-        return held[atom // 16, atom % 16], flat[pl.ds(atom, 1), :]
+        return held[wants_s[slot, t, j + NNB]], flat[pl.ds(wants_s[slot, t, j], 1), :]
 
     for t in range(TASKS):
         for i in range(4):
@@ -320,49 +393,92 @@
             lax.fori_loop(0, 16, three, 0, unroll=True)
             gots[h, c, at, :] = rows_f[5, pl.ds(16 * part, 16), :].astype(BF16)
 
-    done(wheres.at[pl.ds(0, DEVICES - 1)], where_recv)
+    side = pl.ds(pl.multiple_of(64 * c, 64), 64)
+    done(wheres.at[pl.ds(0, DEVICES // 2 - 1)], where_recv)
+    pltpu.make_async_remote_copy(wheres.at[side], wheres.at[side], over_send, over_recv, device_id=sibling, device_id_type=MESH).start()
+    fill_constants(perm)
+    done(wheres.at[pl.ds(0, 64)], over_recv)
     list_ref[...] = slab_list(wheres, (z * SLAB - 3).astype(F32))
 
-    def task(t, carry):
+    def wait_task(t):
         for i in range(4):
             done(got.at[0, 0, pl.ds(0, 16)], z_recv.at[i, t])
             done(gots.at[0, 0, pl.ds(0, 16)], zs_recv.at[i, t])
         done(got.at[0, 0, pl.ds(0, 32)], z_recv.at[4, t])
         done(gots.at[0, 0, pl.ds(0, 32)], zs_recv.at[4, t])
 
+    def assemble_task(t):
         def rows(hh, cc):
-            return jnp.concatenate([gots[hh, cc, pl.ds(pl.multiple_of(64 * part + 16 * t, 16), 16), :] for part in range(2)], axis=0)
-
-        def blocks(g):
-            first = 64 * (g // 2) + 16 * t + 8 * (g % 2)
-            tiles = [
-                jnp.concatenate([got[hh, cc, first + j] for cc in range(2)], axis=1)
-                for j in range(8)
-                for hh in range(2)
-            ]
-            return jnp.concatenate(tiles, axis=0)
-
-        onsite = jnp.concatenate([rows(0, 0), rows(0, 1)], axis=1)
-        ids = rows(1, 0).astype(F32) * 32.0 + rows(1, 1).astype(F32)
-        eye = iota((NNB, NNB), 0) == iota((NNB, NNB), 1)
-        atoms = jnp.sum(jnp.where(eye, atoms_v[pl.ds(t, 1), :].astype(F32), 0.0), axis=1, keepdims=True)
-        density = task_density(atoms, shift_s[t], blocks, onsite, ids, perm, mixed, work)
-        dens_ref[t] = density
+            return jnp.concatenate([gots[hh, cc, pl.ds(pl.multiple_of(64 * part + 16 * t, 16), 16), :] for part in range(2)], axis=0).astype(F32)
+
+        def atoms_of():
+            eye = iota((NNB, NNB), 0) == iota((NNB, NNB), 1)
+            atoms = jnp.sum(jnp.where(eye, atoms_v[pl.ds(t, 1), :].astype(F32), 0.0), axis=1, keepdims=True)
+            return jnp.broadcast_to(atoms, (NNB, 128))
+
+        return assemble(
+            atoms_of,
+            lambda: rows(1, 0) * 32.0 + rows(1, 1),
+            lambda: jnp.concatenate([rows(0, 0), rows(0, 1)], axis=1),
+            lambda j, hh, cc: got[hh, cc, 64 * (j // 16) + 16 * t + j % 16],
+            lambda: shift_s[t], perm, found, mixed, whole, pair, start)
+
+    def iterate_task(t):
+        def set_density(density):
+            dens_ref[t] = density
+
+        def set_box(box):
+            own_box[t] = box
+            boxes_ref[t, slot] = box
+
+        return iterate(start, middle, late, factor, narrow, set_density, lambda: basis_v.at[t], set_box)
+
+    def send_box(t):
+        for_others(lambda peer: pltpu.make_async_remote_copy(own_box.at[t], boxes_ref.at[t, slot], box_send.at[t], box_recv.at[t], device_id=peer, device_id_type=MESH).start())
+
+    def pass_box(t):
+        done(boxes_ref.at[t, pl.ds(0, DEVICES // 2 - 1)], box_recv.at[t])
+        side = pl.ds(64 * c, 64)
+        pltpu.make_async_remote_copy(boxes_ref.at[t, side], boxes_ref.at[t, side], pass_send, pass_recv, device_id=sibling, device_id_type=MESH).start()
+
+    wait_task(0)
+    head, tail = assemble_task(0)
+    for step in head + tail:
+        step()
+
+    def task(t, carry):
+        wait_task(t + 1)
         done(basis_v.at[0], basis_sem.at[t])
-        box = task_box(density, basis_v.at[t])
-        own_box[t] = box
-        boxes_ref[me, t] = box
-        for_others(lambda peer: pltpu.make_async_remote_copy(own_box.at[t], boxes_ref.at[me, t], box_send, box_recv.at[t], device_id=peer, device_id_type=MESH).start())
+        early, rest = iterate_task(t)
+        head, tail = assemble_task(t + 1)
+        steps = early + rest
+        interleaved(steps, head)
+        for step in tail:
+            step()
+        send_box(t)
+
         return carry
 
-    lax.fori_loop(0, TASKS, task, 0)
+    lax.fori_loop(0, TASKS - 1, task, 0)
+    done(basis_v.at[0], basis_sem.at[TASKS - 1])
+    pass_box(0)
+    pass_box(1)
+    early, rest = iterate_task(TASKS - 1)
+    for step in early + rest:
+        step()
+    send_box(TASKS - 1)
+    pass_box(2)
+    pass_box(3)
+    half = pl.ds(0, DEVICES // 2 - 1)
     for t in range(TASKS):
-        done(boxes_ref.at[pl.ds(0, DEVICES - 1), t], box_recv.at[t])
-    done(boxes_ref.at[pl.ds(0, DEVICES - 1)], box_send)
-    done(held.at[pl.ds(0, 2)], sib_send)
-    done(held.at[pl.ds(0, 60)], send_sem)
+        done(boxes_ref.at[t, half], box_send.at[t])
+    for sem in (pass_recv, pass_send):
+        done(boxes_ref.at[pl.ds(0, 2)], sem)
+    done(held.at[pl.ds(0, 34)], sib_send)
+    done(held.at[pl.ds(0, 1020)], send_sem)
     done(wants_v.at[others], want_send)
-    done(wheres.at[pl.ds(0, DEVICES - 1)], where_send)
+    done(wheres.at[pl.ds(0, DEVICES // 2 - 1)], where_send)
+    done(wheres.at[pl.ds(0, 64)], over_send)
     done(to_z, z_send)
     done(to_sib, zs_send.at[0])
     done(rows_z, zs_send.at[1])
@@ -377,13 +493,13 @@
         main_kernel,
         out_shape=(
             jax.ShapeDtypeStruct((TASKS, ORDER, CENTRAL), BF16),
-            jax.ShapeDtypeStruct((DEVICES, TASKS, 8, 128), BF16),
+            jax.ShapeDtypeStruct((TASKS, DEVICES, 8, 128), BF16),
             jax.ShapeDtypeStruct((8, 512), I32),
         ),
         in_specs=[any_space] * 9,
         out_specs=(vmem, vmem, vmem),
         scratch_shapes=[
-            pltpu.VMEM((64, 17, 16, 128), BF16),
+            pltpu.VMEM((64 * 17, 16, 128), BF16),
             pltpu.VMEM((1024, 128), F32),
             pltpu.VMEM((2, 2, 128, 16, 128), BF16),
             pltpu.VMEM((2, 2, 128, 128), BF16),
@@ -397,18 +513,25 @@
             pltpu.VMEM((32, 32), I32),
             pltpu.VMEM((TASKS, NNB), I32),
             pltpu.VMEM((TASKS, ORDER, POINTS), BF16),
-            pltpu.VMEM((5, TASKS, NNB), I32),
-            pltpu.SMEM((6, TASKS, NNB), I32),
+            pltpu.VMEM((6, TASKS, 2 * NNB), I32),
+            pltpu.SMEM((6, TASKS, 2 * NNB), I32),
             pltpu.SMEM((TASKS,), F32),
             pltpu.SMEM((3, TASKS), I32),
             pltpu.VMEM((1, 128), I32),
             pltpu.VMEM((DEVICES, 128), I32),
             pltpu.VMEM((TASKS, 8, 128), BF16),
             pltpu.VMEM((ORDER, ORDER), BF16),
+            pltpu.VMEM((4, 256, 256), BF16),
             pltpu.VMEM((ORDER, ORDER), BF16),
             pltpu.VMEM((ORDER, ORDER), BF16),
-            dma((8,)), dma((TASKS,)), dma((2,)), dma, dma, dma((64,)), dma, dma, dma, dma, dma((5, TASKS)), dma((3,)), dma((5, TASKS)),
-            dma, dma, dma, dma((TASKS,)),
+            pltpu.VMEM((ORDER, ORDER), F32),
+            pltpu.VMEM((ORDER, ORDER), BF16),
+            pltpu.VMEM((ORDER, ORDER), BF16),
+            pltpu.VMEM((ORDER, ORDER), BF16),
+            pltpu.VMEM((ORDER, ORDER), BF16),
+            pltpu.VMEM((ORDER, CENTRAL), BF16),
+            dma((7,)), dma((TASKS,)), dma((2,)), dma, dma, dma((64,)), dma, dma, dma, dma, dma((5, TASKS)), dma((3,)), dma((5, TASKS)),
+            dma, dma, dma, dma, dma((TASKS,)), dma((TASKS,)), dma, dma,
         ],
         compiler_params=pltpu.CompilerParams(collective_id=0, has_side_effects=True, vmem_limit_bytes=56 << 20),
     )(*args)
@@ -424,11 +547,15 @@
         for m in range(4):
             at = 4 * n + m
             start, row, col = list_ref[0, at], list_ref[1, at], list_ref[2, at]
-            box = boxes_ref[list_ref[3, at], list_ref[4, at]].astype(F32)
+            box = boxes_ref[list_ref[4, at], list_ref[3, at]].astype(F32)
             inside = (lane >= col) & (lane < col + 16)
-            for l in range(8):
+            places = [(start + l // 2, pl.ds(row + 8 * (l % 2), 8)) for l in range(8)]
+            sums = []
+            for l, (plane, rows) in enumerate(places):
                 moved = jnp.where(inside, pltpu.roll(box, (col + 128 - 16 * l) % 128, 1), 0.0)
-                grid[start + l // 2, pl.ds(row + 8 * (l % 2), 8), :] += moved
+                sums.append(grid[plane, rows, :] + moved)
+            for (plane, rows), total in zip(places, sums):
+                grid[plane, rows, :] = total
         return carry
 
     lax.fori_loop(0, (list_ref[5, 0] + 3) // 4, add, 0)

time: 81.1 us -> 79.3 us (0.978)
  Pallas kernels: 80.3 us -> 78.4 us
    pallas_call x1, Pallas kernels: 72 us -> 69.4 us  [run_main(): pl.pallas_call(main_kernel, out_shape=(jax.ShapeDtypeStruct((TASKS, ORDER...]
where the time goes in v4:
time: 79.3 us; the launch traced here: 79 us
  Pallas kernels  78.4 us (99%)
    pallas_call x1, Pallas kernels, run_main(): pl.pallas_call(main_kernel, out_shape=(jax.ShapeDtypeStruct((TASKS, ORDER...  69.4 us
    pallas_call x1, Pallas kernels, add_boxes(): pl.pallas_call(add_kernel, out_shape=(jax.ShapeDtypeStruct((SLAB, ROWS, C...  9.02 us

profile of v4, /device:TPU:1, one launch (start us, length us, event | category | flops | bytes accessed | tf_op | source)
XLA Modules:
  0.0 79.0 jit_solution(17812247137789408917)
XLA Ops:
  0.6 69.4 %shard_map.104 = (bf16[4,512,128]{2,1,0:T(8,128)(2,1)}, bf16[4,128,8,128]{3,2,1,0:T(8,128)(2,1)}, s32[8,512]{1,0:T(8,128)}) custom-call(bf16[32,32,256]{2,1,0:T(8,128)(2,1)} %blocks_ref.1, bf16[32,256]{1,0:T(8,128)(2,1)} %onsite_ref.1, s32[32,32]{1,0:T(8,128)} %ids_ref.1, s32[4,32]{1,0:T(4,128)} %atoms_ref.1, f32[4]{0:T(128)} %shift_ref.1, ...), custom_call_target="tpu_custom_call" | custom-call | tf_op jit(solution)/shard_map/pallas_call | solution.py:492
  70.0 9.0 %shard_map.105 = (f32[64,32,128]{2,1,0:T(8,128)}, bf16[4,512,128]{2,1,0:T(8,128)(2,1)}) custom-call(s32[8,512]{1,0:T(8,128)} %get-tuple-element.7.list_ref, bf16[4,128,8,128]{3,2,1,0:T(8,128)(2,1)} %get-tuple-element.8.boxes_ref, bf16[4,512,128]{2,1,0:T(8,128)(2,1)} %get-tuple-element.9.dens_ref), custom_call_target="tpu_custom_call" | custom-call | tf_op jit(solution)/shard_map/pallas_call | solution.py:571

commit v5 on v4

--- a/solution.py
+++ b/solution.py
@@ -189,20 +189,23 @@
         listed += jnp.dot(values.astype(BF16), chosen.astype(F32).astype(BF16), preferred_element_type=F32)
         base = base + totals[:, t : t + 1]
     row, slot = iota((8, 512), 0), iota((8, 512), 1).astype(F32)
-    used = slot < base
-    listed = jnp.where(row == 0, jnp.where(used, listed - first, SLAB + 6.0), listed)
-    return jnp.where(row == 5, base, listed).astype(I32)
+    base_row = (listed[0:1] - first) * ROWS + listed[1:2]
+    lines = [jnp.where(slot[0:1] < base, base_row, (SLAB + 6.0) * ROWS), listed[2:3], listed[4:5] * DEVICES + listed[3:4], base]
+    out = jnp.zeros((8, 512), F32)
+    for v in range(4):
+        out = jnp.where(row == v, lines[v], out)
+    return out.astype(I32)
 
 
 def main_kernel(blocks_ref, onsite_ref, ids_ref, atoms_ref, shift_ref, basis_ref, start_ref, row_ref, col_ref,
                 dens_ref, boxes_ref, list_ref,
                 held, flat, got, gots, to_sib, to_z, rows_f, rows_sib, rows_z, small, onsite_v, ids_v, atoms_v, basis_v,
-                wants_v, wants_s, shift_s, where_s, where_v, wheres, own_box, perm, found, mixed, whole, pair, start, middle, late, factor, narrow,
+                wants_v, wants_s, shift_s, where_s, wheres, perm, found, mixed, whole, pair, start, middle, late, factor, narrow,
                 load_sem, basis_sem, own_sem, sib_send, send_sem, recv_sem, want_send, want_recv, move_sem, z_send, z_recv, zs_send, zs_recv,
-                where_send, where_recv, over_send, over_recv, box_send, box_recv, pass_send, pass_recv):
+                where_send, where_recv, box_send, box_recv):
     y, x, c, z = (lax.axis_index(a) for a in AXES)
     h, o = z % 2, 1 - c
-    slot = c * 64 + (y * 4 + x) * 4 + z
+    slot = c * 64 + y * 16 + x * 4 + z
     sibling = (y, x, o, z)
     up, down = (z + 1) % 4, (z + 3) % 4
     z_peers = [(y, x, c, up), (y, x, o, up), (y, x, c, down), (y, x, o, down)]
@@ -219,17 +222,28 @@
     def done(ref, sem):
         pltpu.make_async_copy(ref, ref, sem).wait()
 
-    def for_others(act, cores=1):
-        def block(b, carry, skip=0):
-            for d in range(skip, 4 * cores):
-                act(((y + b // 4) % 4, (x + b % 4) % 4, (c + d // 4) % 2, (z + d % 4) % 4))
-            return carry
-
-        lax.fori_loop(1, 16, block, 0)
-        block(0, 0, 1)
+    stages = [
+        [(y, x, c, (z + d) % 4) for d in (1, 3, 2)],
+        [(y, (x + d) % 4, c, z) for d in (1, 3, 2)],
+        [((y + d) % 4, x, c, z) for d in (1, 3, 2)],
+        [sibling],
+    ]
+    spans = [(slot, 1), (c * 64 + y * 16 + x * 4, 4), (c * 64 + y * 16, 16), (c * 64, 64)]
+
+    def spread(stage, ref, sends, recvs):
+        first, count = spans[stage]
+        part = ref.at[pl.ds(first, count)]
+        for peer in stages[stage]:
+            pltpu.make_async_remote_copy(part, part, sends.at[stage], recvs.at[stage], device_id=peer, device_id_type=MESH).start()
+
+    def collect(stage, ref, sem):
+        count = spans[stage][1] * len(stages[stage])
+        done(ref.at[pl.ds(0, count)], sem.at[stage])
 
     barrier = pltpu.get_barrier_semaphore()
-    for_others(lambda peer: pl.semaphore_signal(barrier, inc=1, device_id=peer, device_id_type=MESH), 2)
+    peers = stages[0] + stages[1] + stages[2] + stages[3] + [z_peers[1], z_peers[3]]
+    for peer in peers:
+        pl.semaphore_signal(barrier, inc=1, device_id=peer, device_id_type=MESH)
 
     half_k = pl.ds(pl.multiple_of(16 * h, 16), 16)
     mine = pl.ds(pl.multiple_of(128 * c, 128), 128)
@@ -258,7 +272,7 @@
     for f in range(2):
         u = unit(f, 0, 0, c)
         pltpu.make_async_copy(small.at[2 * h + c, f], held.at[17 * u + 16], own_sem.at[f]).start()
-    pl.semaphore_wait(barrier, DEVICES - 1)
+    pl.semaphore_wait(barrier, len(peers))
     for f in range(2):
         u = unit(f, 0, 0, c)
         pltpu.make_async_remote_copy(blocks_ref.at[pl.ds(16 * f, 16), half_k, theirs], held.at[pl.ds(17 * u, 16)], sib_send, recv_sem.at[u], device_id=sibling, device_id_type=MESH).start()
@@ -303,8 +317,8 @@
     for v in range(3):
         for t in range(TASKS):
             where = jnp.where(lane1 == 4 * v + t, where_s[v, t], where)
-    where_v[...] = where
     wheres[pl.ds(slot, 1), :] = where
+    spread(0, wheres, where_send, where_recv)
 
     def take_near(first):
         s = c if first else o
@@ -334,6 +348,8 @@
 
     take_near(True)
     take_near(False)
+    collect(0, wheres, where_recv)
+    spread(1, wheres, where_send, where_recv)
     take_far(0, True)
     take_far(0, False)
     for s in (c, o):
@@ -341,10 +357,13 @@
             u = unit(f, 2, 0, s)
             arrived(u)
             far(f, u)
+    collect(1, wheres, where_recv)
+    spread(2, wheres, where_send, where_recv)
     for dp in (3, 1, 2):
         take_far(dp, True)
         take_far(dp, False)
-    for_others(lambda peer: pltpu.make_async_remote_copy(where_v, wheres.at[pl.ds(slot, 1)], where_send, where_recv, device_id=peer, device_id_type=MESH).start())
+    collect(2, wheres, where_recv)
+    spread(3, wheres, where_send, where_recv)
     others = pl.ds(0, 5)
     done(wants_v.at[others], want_recv)
     moved = pltpu.make_async_copy(wants_v, wants_s, move_sem)
@@ -393,11 +412,8 @@
             lax.fori_loop(0, 16, three, 0, unroll=True)
             gots[h, c, at, :] = rows_f[5, pl.ds(16 * part, 16), :].astype(BF16)
 
-    side = pl.ds(pl.multiple_of(64 * c, 64), 64)
-    done(wheres.at[pl.ds(0, DEVICES // 2 - 1)], where_recv)
-    pltpu.make_async_remote_copy(wheres.at[side], wheres.at[side], over_send, over_recv, device_id=sibling, device_id_type=MESH).start()
     fill_constants(perm)
-    done(wheres.at[pl.ds(0, 64)], over_recv)
+    collect(3, wheres, where_recv)
     list_ref[...] = slab_list(wheres, (z * SLAB - 3).astype(F32))
 
     def wait_task(t):
@@ -428,18 +444,15 @@
             dens_ref[t] = density
 
         def set_box(box):
-            own_box[t] = box
             boxes_ref[t, slot] = box
 
         return iterate(start, middle, late, factor, narrow, set_density, lambda: basis_v.at[t], set_box)
 
-    def send_box(t):
-        for_others(lambda peer: pltpu.make_async_remote_copy(own_box.at[t], boxes_ref.at[t, slot], box_send.at[t], box_recv.at[t], device_id=peer, device_id_type=MESH).start())
-
-    def pass_box(t):
-        done(boxes_ref.at[t, pl.ds(0, DEVICES // 2 - 1)], box_recv.at[t])
-        side = pl.ds(64 * c, 64)
-        pltpu.make_async_remote_copy(boxes_ref.at[t, side], boxes_ref.at[t, side], pass_send, pass_recv, device_id=sibling, device_id_type=MESH).start()
+    def spread_box(stage, t):
+        spread(stage, boxes_ref.at[t], box_send.at[t], box_recv.at[t])
+
+    def collect_box(stage, t):
+        collect(stage, boxes_ref.at[t], box_recv.at[t])
 
     wait_task(0)
     head, tail = assemble_task(0)
@@ -455,30 +468,35 @@
         interleaved(steps, head)
         for step in tail:
             step()
-        send_box(t)
+        spread_box(0, t)
 
         return carry
 
     lax.fori_loop(0, TASKS - 1, task, 0)
     done(basis_v.at[0], basis_sem.at[TASKS - 1])
-    pass_box(0)
-    pass_box(1)
     early, rest = iterate_task(TASKS - 1)
-    for step in early + rest:
+    steps = early + rest
+    earlier = range(TASKS - 1)
+    for n, step in enumerate(steps):
+        if n in (2, 4, 6):
+            stage = n // 2
+            for t in earlier:
+                collect_box(stage - 1, t)
+                spread_box(stage, t)
         step()
-    send_box(TASKS - 1)
-    pass_box(2)
-    pass_box(3)
-    half = pl.ds(0, DEVICES // 2 - 1)
+    spread_box(0, TASKS - 1)
+    for stage in range(1, 4):
+        collect_box(stage - 1, TASKS - 1)
+        spread_box(stage, TASKS - 1)
     for t in range(TASKS):
-        done(boxes_ref.at[t, half], box_send.at[t])
-    for sem in (pass_recv, pass_send):
-        done(boxes_ref.at[pl.ds(0, 2)], sem)
+        collect_box(3, t)
+        for stage in range(4):
+            collect(stage, boxes_ref.at[t], box_send.at[t])
     done(held.at[pl.ds(0, 34)], sib_send)
     done(held.at[pl.ds(0, 1020)], send_sem)
     done(wants_v.at[others], want_send)
-    done(wheres.at[pl.ds(0, DEVICES // 2 - 1)], where_send)
-    done(wheres.at[pl.ds(0, 64)], over_send)
+    for stage in range(4):
+        collect(stage, wheres, where_send)
     done(to_z, z_send)
     done(to_sib, zs_send.at[0])
     done(rows_z, zs_send.at[1])
@@ -517,9 +535,7 @@
             pltpu.SMEM((6, TASKS, 2 * NNB), I32),
             pltpu.SMEM((TASKS,), F32),
             pltpu.SMEM((3, TASKS), I32),
-            pltpu.VMEM((1, 128), I32),
             pltpu.VMEM((DEVICES, 128), I32),
-            pltpu.VMEM((TASKS, 8, 128), BF16),
             pltpu.VMEM((ORDER, ORDER), BF16),
             pltpu.VMEM((4, 256, 256), BF16),
             pltpu.VMEM((ORDER, ORDER), BF16),
@@ -531,7 +547,7 @@
             pltpu.VMEM((ORDER, ORDER), BF16),
             pltpu.VMEM((ORDER, CENTRAL), BF16),
             dma((7,)), dma((TASKS,)), dma((2,)), dma, dma, dma((64,)), dma, dma, dma, dma, dma((5, TASKS)), dma((3,)), dma((5, TASKS)),
-            dma, dma, dma, dma, dma((TASKS,)), dma((TASKS,)), dma, dma,
+            dma((4,)), dma((4,)), dma((TASKS, 4)), dma((TASKS, 4)),
         ],
         compiler_params=pltpu.CompilerParams(collective_id=0, has_side_effects=True, vmem_limit_bytes=56 << 20),
     )(*args)
@@ -546,20 +562,19 @@
     def add(n, carry):
         for m in range(4):
             at = 4 * n + m
-            start, row, col = list_ref[0, at], list_ref[1, at], list_ref[2, at]
-            box = boxes_ref[list_ref[4, at], list_ref[3, at]].astype(F32)
+            base, col = list_ref[0, at], list_ref[1, at]
+            turned = pltpu.roll(boxes_ref[list_ref[2, at]].astype(F32), col, 1)
             inside = (lane >= col) & (lane < col + 16)
-            places = [(start + l // 2, pl.ds(row + 8 * (l % 2), 8)) for l in range(8)]
             sums = []
-            for l, (plane, rows) in enumerate(places):
-                moved = jnp.where(inside, pltpu.roll(box, (col + 128 - 16 * l) % 128, 1), 0.0)
-                sums.append(grid[plane, rows, :] + moved)
-            for (plane, rows), total in zip(places, sums):
-                grid[plane, rows, :] = total
+            for l in range(8):
+                moved = pltpu.roll(turned, 128 - 16 * l, 1) if l else turned
+                sums.append(grid[pl.ds(base + 16 * l - 8 * (l % 2), 8), :] + jnp.where(inside, moved, 0.0))
+            for l in range(8):
+                grid[pl.ds(base + 16 * l - 8 * (l % 2), 8), :] = sums[l]
         return carry
 
-    lax.fori_loop(0, (list_ref[5, 0] + 3) // 4, add, 0)
-    copy = pltpu.make_async_copy(grid.at[pl.ds(3, SLAB)], out_ref, sem)
+    lax.fori_loop(0, (list_ref[3, 0] + 3) // 4, add, 0)
+    copy = pltpu.make_async_copy(grid.at[pl.ds(3 * ROWS, SLAB * ROWS)], out_ref, sem)
     copy.start()
     copy.wait()
     through.wait()
@@ -571,13 +586,13 @@
     return pl.pallas_call(
         add_kernel,
         out_shape=(
-            jax.ShapeDtypeStruct((SLAB, ROWS, COLS), F32),
+            jax.ShapeDtypeStruct((SLAB * ROWS, COLS), F32),
             jax.ShapeDtypeStruct(dens.shape, dens.dtype),
         ),
         in_specs=[pl.BlockSpec(memory_space=pltpu.SMEM), vmem, vmem],
         out_specs=(any_space, any_space),
         scratch_shapes=[
-            pltpu.VMEM((SLAB + 10, ROWS, COLS), F32),
+            pltpu.VMEM(((SLAB + 10) * ROWS, COLS), F32),
             pltpu.SemaphoreType.DMA,
             pltpu.SemaphoreType.DMA,
         ],
@@ -586,8 +601,8 @@
 
 def on_device(*args):
     dens, boxes, listed = run_main(*args)
-    rho, dens = add_boxes(listed, boxes, dens)
-    return dens, rho
+    rho, dens = add_boxes(listed, boxes.reshape(TASKS * DEVICES, 8, 128), dens)
+    return dens, rho.reshape(SLAB, ROWS, COLS)
 
 
 def solution(mesh):

time: 79.3 us -> 86 us (1.084)
  Pallas kernels: 78.4 us -> 84.6 us
    pallas_call x1, Pallas kernels: 69.4 us -> 76.9 us  [run_main(): pl.pallas_call(main_kernel, out_shape=(jax.ShapeDtypeStruct((TASKS, ORDER...]
    pallas_call x1, Pallas kernels: 9.02 us -> 7.68 us  [add_boxes(): pl.pallas_call(add_kernel, out_shape=(jax.ShapeDtypeStruct((SLAB * ROWS,...]
where the time goes in v5:
time: 86 us; the launch traced here: 85.2 us
  Pallas kernels  84.6 us (98%)
    pallas_call x1, Pallas kernels, run_main(): pl.pallas_call(main_kernel, out_shape=(jax.ShapeDtypeStruct((TASKS, ORDER...  76.9 us
    pallas_call x1, Pallas kernels, add_boxes(): pl.pallas_call(add_kernel, out_shape=(jax.ShapeDtypeStruct((SLAB * ROWS,...  7.68 us

profile of v5, /device:TPU:1, one launch (start us, length us, event | category | flops | bytes accessed | tf_op | source)
XLA Modules:
  0.0 85.2 jit_solution(1777901754094437913)
XLA Ops:
  0.6 76.9 %shard_map.104 = (bf16[4,512,128]{2,1,0:T(8,128)(2,1)}, bf16[4,128,8,128]{3,2,1,0:T(8,128)(2,1)}, s32[8,512]{1,0:T(8,128)}) custom-call(bf16[32,32,256]{2,1,0:T(8,128)(2,1)} %blocks_ref.1, bf16[32,256]{1,0:T(8,128)(2,1)} %onsite_ref.1, s32[32,32]{1,0:T(8,128)} %ids_ref.1, s32[4,32]{1,0:T(4,128)} %atoms_ref.1, f32[4]{0:T(128)} %shift_ref.1, ...), custom_call_target="tpu_custom_call" | custom-call | tf_op jit(solution)/shard_map/pallas_call | solution.py:510
  77.6 7.7 %shard_map.105 = (f32[2048,128]{1,0:T(8,128)}, bf16[4,512,128]{2,1,0:T(8,128)(2,1)}) custom-call(s32[8,512]{1,0:T(8,128)} %get-tuple-element.7.list_ref, bf16[512,8,128]{2,1,0:T(8,128)(2,1)} %bitcast.2, bf16[4,512,128]{2,1,0:T(8,128)(2,1)} %get-tuple-element.9.dens_ref), custom_call_target="tpu_custom_call" | custom-call | tf_op jit(solution)/shard_map/pallas_call | solution.py:586

commit v6 on v4

--- a/solution.py
+++ b/solution.py
@@ -8,8 +8,8 @@
 
 F32, BF16, I32 = jnp.float32, jnp.bfloat16, jnp.int32
 BS, KNB, NNB, ORDER, CENTRAL, POINTS, ITERS = 16, 32, 32, 512, 128, 1024, 3
-SLAB, ROWS, COLS = 64, 32, 128
-DEVICES, TASKS = 128, 4
+SLAB, ROWS, COLS, BOXP = 64, 32, 128, 4
+DEVICES, TASKS, TOGETHER = 128, 4, 16
 AXES = ("atoms_0", "atoms_1", "atoms_2", "grid")
 MESH = pl.DeviceIdType.MESH
 
@@ -189,20 +189,30 @@
         listed += jnp.dot(values.astype(BF16), chosen.astype(F32).astype(BF16), preferred_element_type=F32)
         base = base + totals[:, t : t + 1]
     row, slot = iota((8, 512), 0), iota((8, 512), 1).astype(F32)
-    used = slot < base
-    listed = jnp.where(row == 0, jnp.where(used, listed - first, SLAB + 6.0), listed)
-    return jnp.where(row == 5, base, listed).astype(I32)
+    eights = jnp.floor(listed[1:2] * 0.125) * 8.0
+    base_row = (listed[0:1] - first) * ROWS + eights
+    lines = [
+        jnp.where(slot[0:1] < base, base_row, (SLAB + 6.0) * ROWS),
+        listed[2:3],
+        listed[4:5] * DEVICES + listed[3:4],
+        base,
+        listed[1:2] - eights,
+    ]
+    out = jnp.zeros((8, 512), F32)
+    for v, values in enumerate(lines):
+        out = jnp.where(row == v, values, out)
+    return out.astype(I32)
 
 
 def main_kernel(blocks_ref, onsite_ref, ids_ref, atoms_ref, shift_ref, basis_ref, start_ref, row_ref, col_ref,
                 dens_ref, boxes_ref, list_ref,
                 held, flat, got, gots, to_sib, to_z, rows_f, rows_sib, rows_z, small, onsite_v, ids_v, atoms_v, basis_v,
-                wants_v, wants_s, shift_s, where_s, where_v, wheres, own_box, perm, found, mixed, whole, pair, start, middle, late, factor, narrow,
-                load_sem, basis_sem, own_sem, sib_send, send_sem, recv_sem, want_send, want_recv, move_sem, z_send, z_recv, zs_send, zs_recv,
-                where_send, where_recv, over_send, over_recv, box_send, box_recv, pass_send, pass_recv):
+                wants_v, wants_s, shift_s, where_s, where_v, wheres, perm, found, mixed, whole, pair, start, middle, late, factor, narrow,
+                load_sem, basis_sem, own_sem, sib_send, send_sem, recv_sem, want_send, want_recv, move_sem, here_sem, z_send, z_recv, zs_send, zs_recv,
+                where_send, where_recv, over_send, over_recv, box_send, box_recv):
     y, x, c, z = (lax.axis_index(a) for a in AXES)
     h, o = z % 2, 1 - c
-    slot = c * 64 + (y * 4 + x) * 4 + z
+    slot = c * 64 + y * 16 + x * 4 + z
     sibling = (y, x, o, z)
     up, down = (z + 1) % 4, (z + 3) % 4
     z_peers = [(y, x, c, up), (y, x, o, up), (y, x, c, down), (y, x, o, down)]
@@ -229,7 +239,23 @@
         block(0, 0, 1)
 
     barrier = pltpu.get_barrier_semaphore()
-    for_others(lambda peer: pl.semaphore_signal(barrier, inc=1, device_id=peer, device_id_type=MESH), 2)
+    near = [
+        [(y, x, c, (z + d) % 4) for d in (1, 3, 2)],
+        [(y, (x + d) % 4, c, z) for d in (1, 3, 2)],
+        [((y + d) % 4, x, c, z) for d in (1, 3, 2)],
+        [sibling],
+    ]
+    peers = near[0] + near[1] + near[2] + near[3] + [z_peers[1], z_peers[3]]
+    for peer in peers:
+        pl.semaphore_signal(barrier, inc=1, device_id=peer, device_id_type=MESH)
+
+    def tell(stage):
+        for peer in near[stage]:
+            pl.semaphore_signal(here_sem.at[stage], inc=1, device_id=peer, device_id_type=MESH)
+
+    def told(stage):
+        pl.semaphore_wait(here_sem.at[stage], len(near[stage]))
+
 
     half_k = pl.ds(pl.multiple_of(16 * h, 16), 16)
     mine = pl.ds(pl.multiple_of(128 * c, 128), 128)
@@ -258,7 +284,8 @@
     for f in range(2):
         u = unit(f, 0, 0, c)
         pltpu.make_async_copy(small.at[2 * h + c, f], held.at[17 * u + 16], own_sem.at[f]).start()
-    pl.semaphore_wait(barrier, DEVICES - 1)
+    pl.semaphore_wait(barrier, len(peers))
+    tell(0)
     for f in range(2):
         u = unit(f, 0, 0, c)
         pltpu.make_async_remote_copy(blocks_ref.at[pl.ds(16 * f, 16), half_k, theirs], held.at[pl.ds(17 * u, 16)], sib_send, recv_sem.at[u], device_id=sibling, device_id_type=MESH).start()
@@ -270,7 +297,7 @@
     def arrived(u):
         done(held.at[pl.ds(17 * u, 17)], recv_sem.at[u])
 
-    def near(f, u):
+    def beside(f, u):
         send(f, u, 1, 0)
         send(f, u, 3, 0)
 
@@ -281,11 +308,11 @@
     for f in range(2):
         u = unit(f, 0, 0, c)
         done(held.at[pl.ds(17 * u, 17)], own_sem.at[f])
-        near(f, u)
+        beside(f, u)
     for f in range(2):
         u = unit(f, 0, 0, o)
         arrived(u)
-        near(f, u)
+        beside(f, u)
     for s in (c, o):
         for f in range(2):
             far(f, unit(f, 0, 0, s))
@@ -333,9 +360,16 @@
                 send(f, u, 0, 3)
 
     take_near(True)
+    told(0)
+    tell(1)
     take_near(False)
+    told(1)
+    tell(2)
     take_far(0, True)
+    told(2)
+    tell(3)
     take_far(0, False)
+    told(3)
     for s in (c, o):
         for f in range(2):
             u = unit(f, 2, 0, s)
@@ -428,18 +462,17 @@
             dens_ref[t] = density
 
         def set_box(box):
-            own_box[t] = box
             boxes_ref[t, slot] = box
 
         return iterate(start, middle, late, factor, narrow, set_density, lambda: basis_v.at[t], set_box)
 
-    def send_box(t):
-        for_others(lambda peer: pltpu.make_async_remote_copy(own_box.at[t], boxes_ref.at[t, slot], box_send.at[t], box_recv.at[t], device_id=peer, device_id_type=MESH).start())
-
-    def pass_box(t):
-        done(boxes_ref.at[t, pl.ds(0, DEVICES // 2 - 1)], box_recv.at[t])
-        side = pl.ds(64 * c, 64)
-        pltpu.make_async_remote_copy(boxes_ref.at[t, side], boxes_ref.at[t, side], pass_send, pass_recv, device_id=sibling, device_id_type=MESH).start()
+    def send_box(part, peer, t, stage):
+        pltpu.make_async_remote_copy(boxes_ref.at[t, part], boxes_ref.at[t, part], box_send.at[t, stage], box_recv.at[t, stage], device_id=peer, device_id_type=MESH).start()
+
+    def box_done(t, stage, count, sem):
+        done(boxes_ref.at[t, pl.ds(0, count)], sem.at[t, stage])
+
+    z_span = pl.ds(c * 64 + y * 16 + x * 4, 4)
 
     wait_task(0)
     head, tail = assemble_task(0)
@@ -455,25 +488,31 @@
         interleaved(steps, head)
         for step in tail:
             step()
-        send_box(t)
+        for d in (1, 3, 2):
+            send_box(pl.ds(slot, 1), (y, x, c, (z + d) % 4), t, 0)
 
         return carry
 
     lax.fori_loop(0, TASKS - 1, task, 0)
     done(basis_v.at[0], basis_sem.at[TASKS - 1])
-    pass_box(0)
-    pass_box(1)
+    for t in range(TASKS - 1):
+        box_done(t, 0, 3, box_recv)
+        for d in range(1, 16):
+            send_box(z_span, ((y + d // 4) % 4, (x + d % 4) % 4, c, z), t, 1)
     early, rest = iterate_task(TASKS - 1)
     for step in early + rest:
         step()
-    send_box(TASKS - 1)
-    pass_box(2)
-    pass_box(3)
-    half = pl.ds(0, DEVICES // 2 - 1)
-    for t in range(TASKS):
-        done(boxes_ref.at[t, half], box_send.at[t])
-    for sem in (pass_recv, pass_send):
-        done(boxes_ref.at[pl.ds(0, 2)], sem)
+    for_others(lambda peer: send_box(pl.ds(slot, 1), peer, TASKS - 1, 0), 2)
+    for t in range(TASKS - 1):
+        box_done(t, 1, 60, box_recv)
+        send_box(pl.ds(c * 64, 64), sibling, t, 2)
+    for t in range(TASKS - 1):
+        box_done(t, 2, 64, box_recv)
+        box_done(t, 0, 3, box_send)
+        box_done(t, 1, 60, box_send)
+        box_done(t, 2, 64, box_send)
+    box_done(TASKS - 1, 0, DEVICES - 1, box_recv)
+    box_done(TASKS - 1, 0, DEVICES - 1, box_send)
     done(held.at[pl.ds(0, 34)], sib_send)
     done(held.at[pl.ds(0, 1020)], send_sem)
     done(wants_v.at[others], want_send)
@@ -519,7 +558,6 @@
             pltpu.SMEM((3, TASKS), I32),
             pltpu.VMEM((1, 128), I32),
             pltpu.VMEM((DEVICES, 128), I32),
-            pltpu.VMEM((TASKS, 8, 128), BF16),
             pltpu.VMEM((ORDER, ORDER), BF16),
             pltpu.VMEM((4, 256, 256), BF16),
             pltpu.VMEM((ORDER, ORDER), BF16),
@@ -530,8 +568,8 @@
             pltpu.VMEM((ORDER, ORDER), BF16),
             pltpu.VMEM((ORDER, ORDER), BF16),
             pltpu.VMEM((ORDER, CENTRAL), BF16),
-            dma((7,)), dma((TASKS,)), dma((2,)), dma, dma, dma((64,)), dma, dma, dma, dma, dma((5, TASKS)), dma((3,)), dma((5, TASKS)),
-            dma, dma, dma, dma, dma((TASKS,)), dma((TASKS,)), dma, dma,
+            dma((7,)), dma((TASKS,)), dma((2,)), dma, dma, dma((64,)), dma, dma, dma, pltpu.SemaphoreType.REGULAR((4,)), dma, dma((5, TASKS)), dma((3,)), dma((5, TASKS)),
+            dma, dma, dma, dma, dma((TASKS, 3)), dma((TASKS, 3)),
         ],
         compiler_params=pltpu.CompilerParams(collective_id=0, has_side_effects=True, vmem_limit_bytes=56 << 20),
     )(*args)
@@ -543,23 +581,33 @@
     grid[...] = jnp.zeros_like(grid)
     lane = iota((8, 128), 1)
 
+    line = iota((8, 128), 0)
+
     def add(n, carry):
-        for m in range(4):
-            at = 4 * n + m
-            start, row, col = list_ref[0, at], list_ref[1, at], list_ref[2, at]
-            box = boxes_ref[list_ref[4, at], list_ref[3, at]].astype(F32)
+        for m in range(TOGETHER):
+            at = TOGETHER * n + m
+            base, col, down = pl.multiple_of(list_ref[0, at], 8), list_ref[1, at], list_ref[4, at]
+            turned = pltpu.roll(pltpu.roll(boxes_ref[list_ref[2, at]].astype(F32), col, 1), down, 0)
             inside = (lane >= col) & (lane < col + 16)
-            places = [(start + l // 2, pl.ds(row + 8 * (l % 2), 8)) for l in range(8)]
-            sums = []
-            for l, (plane, rows) in enumerate(places):
-                moved = jnp.where(inside, pltpu.roll(box, (col + 128 - 16 * l) % 128, 1), 0.0)
-                sums.append(grid[plane, rows, :] + moved)
-            for (plane, rows), total in zip(places, sums):
-                grid[plane, rows, :] = total
+            upper, lower = inside & (line >= down), inside & (line < down)
+            pieces = [pltpu.roll(turned, 128 - 16 * l, 1) if l else turned for l in range(8)]
+            sums = {}
+            for k in range(BOXP):
+                first, second = pieces[2 * k], pieces[2 * k + 1]
+                parts = [
+                    jnp.where(upper, first, 0.0),
+                    jnp.where(upper, second, jnp.where(lower, first, 0.0)),
+                    jnp.where(lower, second, 0.0),
+                ]
+                for n8, part in enumerate(parts):
+                    off = ROWS * k + 8 * n8
+                    sums[off] = grid[pl.ds(base + off, 8), :] + part
+            for off, total in sums.items():
+                grid[pl.ds(base + off, 8), :] = total
         return carry
 
-    lax.fori_loop(0, (list_ref[5, 0] + 3) // 4, add, 0)
-    copy = pltpu.make_async_copy(grid.at[pl.ds(3, SLAB)], out_ref, sem)
+    lax.fori_loop(0, (list_ref[3, 0] + TOGETHER - 1) // TOGETHER, add, 0)
+    copy = pltpu.make_async_copy(grid.at[pl.ds(3 * ROWS, SLAB * ROWS)], out_ref, sem)
     copy.start()
     copy.wait()
     through.wait()
@@ -571,13 +619,13 @@
     return pl.pallas_call(
         add_kernel,
         out_shape=(
-            jax.ShapeDtypeStruct((SLAB, ROWS, COLS), F32),
+            jax.ShapeDtypeStruct((SLAB * ROWS, COLS), F32),
             jax.ShapeDtypeStruct(dens.shape, dens.dtype),
         ),
         in_specs=[pl.BlockSpec(memory_space=pltpu.SMEM), vmem, vmem],
         out_specs=(any_space, any_space),
         scratch_shapes=[
-            pltpu.VMEM((SLAB + 10, ROWS, COLS), F32),
+            pltpu.VMEM(((SLAB + 10) * ROWS, COLS), F32),
             pltpu.SemaphoreType.DMA,
             pltpu.SemaphoreType.DMA,
         ],
@@ -586,8 +634,8 @@
 
 def on_device(*args):
     dens, boxes, listed = run_main(*args)
-    rho, dens = add_boxes(listed, boxes, dens)
-    return dens, rho
+    rho, dens = add_boxes(listed, boxes.reshape(TASKS * DEVICES, 8, 128), dens)
+    return dens, rho.reshape(SLAB, ROWS, COLS)
 
 
 def solution(mesh):

time: 79.3 us -> 72.4 us (0.913)
  Pallas kernels: 78.4 us -> 71.5 us
    pallas_call x1, Pallas kernels: 9.02 us -> 5.45 us  [add_boxes(): pl.pallas_call(add_kernel, out_shape=(jax.ShapeDtypeStruct((SLAB * ROWS,...]
    pallas_call x1, Pallas kernels: 69.4 us -> 66 us  [run_main(): pl.pallas_call(main_kernel, out_shape=(jax.ShapeDtypeStruct((TASKS, ORDER...]
where the time goes in v6:
time: 72.4 us; the launch traced here: 72.1 us
  Pallas kernels  71.5 us (99%)
    pallas_call x1, Pallas kernels, run_main(): pl.pallas_call(main_kernel, out_shape=(jax.ShapeDtypeStruct((TASKS, ORDER...  66 us
    pallas_call x1, Pallas kernels, add_boxes(): pl.pallas_call(add_kernel, out_shape=(jax.ShapeDtypeStruct((SLAB * ROWS,...  5.45 us

profile of v6, /device:TPU:1, one launch (start us, length us, event | category | flops | bytes accessed | tf_op | source)
XLA Modules:
  0.0 72.1 jit_solution(2560051156941021640)
XLA Ops:
  0.6 66.0 %shard_map.104 = (bf16[4,512,128]{2,1,0:T(8,128)(2,1)}, bf16[4,128,8,128]{3,2,1,0:T(8,128)(2,1)}, s32[8,512]{1,0:T(8,128)}) custom-call(bf16[32,32,256]{2,1,0:T(8,128)(2,1)} %blocks_ref.1, bf16[32,256]{1,0:T(8,128)(2,1)} %onsite_ref.1, s32[32,32]{1,0:T(8,128)} %ids_ref.1, s32[4,32]{1,0:T(4,128)} %atoms_ref.1, f32[4]{0:T(128)} %shift_ref.1, ...), custom_call_target="tpu_custom_call" | custom-call | tf_op jit(solution)/shard_map/pallas_call | solution.py:531
  66.7 5.5 %shard_map.105 = (f32[2048,128]{1,0:T(8,128)}, bf16[4,512,128]{2,1,0:T(8,128)(2,1)}) custom-call(s32[8,512]{1,0:T(8,128)} %get-tuple-element.7.list_ref, bf16[512,8,128]{2,1,0:T(8,128)(2,1)} %bitcast.2, bf16[4,512,128]{2,1,0:T(8,128)(2,1)} %get-tuple-element.9.dens_ref), custom_call_target="tpu_custom_call" | custom-call | tf_op jit(solution)/shard_map/pallas_call | solution.py:619

commit v7 on v6

--- a/solution.py
+++ b/solution.py
@@ -9,7 +9,7 @@
 F32, BF16, I32 = jnp.float32, jnp.bfloat16, jnp.int32
 BS, KNB, NNB, ORDER, CENTRAL, POINTS, ITERS = 16, 32, 32, 512, 128, 1024, 3
 SLAB, ROWS, COLS, BOXP = 64, 32, 128, 4
-DEVICES, TASKS, TOGETHER = 128, 4, 16
+DEVICES, TASKS, TOGETHER, LISTED = 128, 4, 24, 640
 AXES = ("atoms_0", "atoms_1", "atoms_2", "grid")
 MESH = pl.DeviceIdType.MESH
 
@@ -176,9 +176,9 @@
     before = jnp.dot(below, hit.astype(BF16), preferred_element_type=F32)
     totals = jnp.sum(hit, axis=0, keepdims=True)
     turned = rows.T
-    slots = iota((DEVICES, 512), 1).astype(F32)
+    slots = iota((DEVICES, LISTED), 1).astype(F32)
     base = jnp.zeros((1, 1), F32)
-    listed = jnp.zeros((8, 512), F32)
+    listed = jnp.zeros((8, LISTED), F32)
     line = iota((8, 128), 0)
     device = iota((8, 128), 1).astype(F32)
     for t in range(TASKS):
@@ -188,7 +188,7 @@
             values = jnp.where(line == v, turned[4 * v + t : 4 * v + t + 1, :], values)
         listed += jnp.dot(values.astype(BF16), chosen.astype(F32).astype(BF16), preferred_element_type=F32)
         base = base + totals[:, t : t + 1]
-    row, slot = iota((8, 512), 0), iota((8, 512), 1).astype(F32)
+    row, slot = iota((8, LISTED), 0), iota((8, LISTED), 1).astype(F32)
     eights = jnp.floor(listed[1:2] * 0.125) * 8.0
     base_row = (listed[0:1] - first) * ROWS + eights
     lines = [
@@ -198,7 +198,7 @@
         base,
         listed[1:2] - eights,
     ]
-    out = jnp.zeros((8, 512), F32)
+    out = jnp.zeros((8, LISTED), F32)
     for v, values in enumerate(lines):
         out = jnp.where(row == v, values, out)
     return out.astype(I32)
@@ -383,6 +383,7 @@
     done(wants_v.at[others], want_recv)
     moved = pltpu.make_async_copy(wants_v, wants_s, move_sem)
     moved.start()
+    fill_constants(perm)
     for dp in range(4):
         for f in range(2):
             for s in (c, o):
@@ -430,7 +431,6 @@
     side = pl.ds(pl.multiple_of(64 * c, 64), 64)
     done(wheres.at[pl.ds(0, DEVICES // 2 - 1)], where_recv)
     pltpu.make_async_remote_copy(wheres.at[side], wheres.at[side], over_send, over_recv, device_id=sibling, device_id_type=MESH).start()
-    fill_constants(perm)
     done(wheres.at[pl.ds(0, 64)], over_recv)
     list_ref[...] = slab_list(wheres, (z * SLAB - 3).astype(F32))
 
@@ -495,12 +495,14 @@
 
     lax.fori_loop(0, TASKS - 1, task, 0)
     done(basis_v.at[0], basis_sem.at[TASKS - 1])
+    early, rest = iterate_task(TASKS - 1)
+    for step in early + rest[:2]:
+        step()
     for t in range(TASKS - 1):
         box_done(t, 0, 3, box_recv)
         for d in range(1, 16):
             send_box(z_span, ((y + d // 4) % 4, (x + d % 4) % 4, c, z), t, 1)
-    early, rest = iterate_task(TASKS - 1)
-    for step in early + rest:
+    for step in rest[2:]:
         step()
     for_others(lambda peer: send_box(pl.ds(slot, 1), peer, TASKS - 1, 0), 2)
     for t in range(TASKS - 1):
@@ -533,7 +535,7 @@
         out_shape=(
             jax.ShapeDtypeStruct((TASKS, ORDER, CENTRAL), BF16),
             jax.ShapeDtypeStruct((TASKS, DEVICES, 8, 128), BF16),
-            jax.ShapeDtypeStruct((8, 512), I32),
+            jax.ShapeDtypeStruct((8, LISTED), I32),
         ),
         in_specs=[any_space] * 9,
         out_specs=(vmem, vmem, vmem),

time: 72.4 us -> 71.5 us (0.988)
  Pallas kernels: 71.5 us -> 70.7 us
where the time goes in v7:
time: 71.5 us; the launch traced here: 71.3 us
  Pallas kernels  70.7 us (99%)
    pallas_call x1, Pallas kernels, run_main(): pl.pallas_call(main_kernel, out_shape=(jax.ShapeDtypeStruct((TASKS, ORDER...  65.7 us
    pallas_call x1, Pallas kernels, add_boxes(): pl.pallas_call(add_kernel, out_shape=(jax.ShapeDtypeStruct((SLAB * ROWS,...  5.01 us

profile of v7, /device:TPU:1, one launch (start us, length us, event | category | flops | bytes accessed | tf_op | source)
XLA Modules:
  0.0 71.3 jit_solution(13195554439210305144)
XLA Ops:
  0.6 65.7 %shard_map.104 = (bf16[4,512,128]{2,1,0:T(8,128)(2,1)}, bf16[4,128,8,128]{3,2,1,0:T(8,128)(2,1)}, s32[8,640]{1,0:T(8,128)}) custom-call(bf16[32,32,256]{2,1,0:T(8,128)(2,1)} %blocks_ref.1, bf16[32,256]{1,0:T(8,128)(2,1)} %onsite_ref.1, s32[32,32]{1,0:T(8,128)} %ids_ref.1, s32[4,32]{1,0:T(4,128)} %atoms_ref.1, f32[4]{0:T(128)} %shift_ref.1, ...), custom_call_target="tpu_custom_call" | custom-call | tf_op jit(solution)/shard_map/pallas_call | solution.py:533
  66.3 5.0 %shard_map.105 = (f32[2048,128]{1,0:T(8,128)}, bf16[4,512,128]{2,1,0:T(8,128)(2,1)}) custom-call(s32[8,640]{1,0:T(8,128)} %get-tuple-element.7.list_ref, bf16[512,8,128]{2,1,0:T(8,128)(2,1)} %bitcast.2, bf16[4,512,128]{2,1,0:T(8,128)(2,1)} %get-tuple-element.9.dens_ref), custom_call_target="tpu_custom_call" | custom-call | tf_op jit(solution)/shard_map/pallas_call | solution.py:621

commit v8 on v7

--- a/solution.py
+++ b/solution.py
@@ -310,12 +310,13 @@
         done(held.at[pl.ds(17 * u, 17)], own_sem.at[f])
         beside(f, u)
     for f in range(2):
+        far(f, unit(f, 0, 0, c))
+    for f in range(2):
         u = unit(f, 0, 0, o)
         arrived(u)
         beside(f, u)
-    for s in (c, o):
-        for f in range(2):
-            far(f, unit(f, 0, 0, s))
+    for f in range(2):
+        far(f, unit(f, 0, 0, o))
     for load in loads[2:]:
         load.wait()
     for i in range(TASKS):
@@ -431,8 +432,6 @@
     side = pl.ds(pl.multiple_of(64 * c, 64), 64)
     done(wheres.at[pl.ds(0, DEVICES // 2 - 1)], where_recv)
     pltpu.make_async_remote_copy(wheres.at[side], wheres.at[side], over_send, over_recv, device_id=sibling, device_id_type=MESH).start()
-    done(wheres.at[pl.ds(0, 64)], over_recv)
-    list_ref[...] = slab_list(wheres, (z * SLAB - 3).astype(F32))
 
     def wait_task(t):
         for i in range(4):
@@ -505,6 +504,8 @@
     for step in rest[2:]:
         step()
     for_others(lambda peer: send_box(pl.ds(slot, 1), peer, TASKS - 1, 0), 2)
+    done(wheres.at[pl.ds(0, 64)], over_recv)
+    list_ref[...] = slab_list(wheres, (z * SLAB - 3).astype(F32))
     for t in range(TASKS - 1):
         box_done(t, 1, 60, box_recv)
         send_box(pl.ds(c * 64, 64), sibling, t, 2)

time: 71.5 us -> 71.5 us (level)
  no operation moved by 1% of the time
where the time goes in v8:
time: 71.5 us; the launch traced here: 71.3 us
  Pallas kernels  70.7 us (99%)
    pallas_call x1, Pallas kernels, run_main(): pl.pallas_call(main_kernel, out_shape=(jax.ShapeDtypeStruct((TASKS, ORDER...  65.6 us
    pallas_call x1, Pallas kernels, add_boxes(): pl.pallas_call(add_kernel, out_shape=(jax.ShapeDtypeStruct((SLAB * ROWS,...  5.01 us

profile of v8, /device:TPU:1, one launch (start us, length us, event | category | flops | bytes accessed | tf_op | source)
XLA Modules:
  0.0 71.3 jit_solution(15694613189264236705)
XLA Ops:
  0.6 65.6 %shard_map.104 = (bf16[4,512,128]{2,1,0:T(8,128)(2,1)}, bf16[4,128,8,128]{3,2,1,0:T(8,128)(2,1)}, s32[8,640]{1,0:T(8,128)}) custom-call(bf16[32,32,256]{2,1,0:T(8,128)(2,1)} %blocks_ref.1, bf16[32,256]{1,0:T(8,128)(2,1)} %onsite_ref.1, s32[32,32]{1,0:T(8,128)} %ids_ref.1, s32[4,32]{1,0:T(4,128)} %atoms_ref.1, f32[4]{0:T(128)} %shift_ref.1, ...), custom_call_target="tpu_custom_call" | custom-call | tf_op jit(solution)/shard_map/pallas_call | solution.py:534
  66.3 5.0 %shard_map.105 = (f32[2048,128]{1,0:T(8,128)}, bf16[4,512,128]{2,1,0:T(8,128)(2,1)}) custom-call(s32[8,640]{1,0:T(8,128)} %get-tuple-element.7.list_ref, bf16[512,8,128]{2,1,0:T(8,128)(2,1)} %bitcast.2, bf16[4,512,128]{2,1,0:T(8,128)(2,1)} %get-tuple-element.9.dens_ref), custom_call_target="tpu_custom_call" | custom-call | tf_op jit(solution)/shard_map/pallas_call | solution.py:622
